TPU v7x, 128 devices: a whole 4x4x4 slice. The times are simulated.
128 devices in a mesh: seq: 64 (over x, z, y), head: 2 (over core).
Axes of the slice: x: 4, y: 4, z: 4, core: 2. Of those that a mesh axis runs over, the one named last changes fastest.
Arguments:
- queries: bfloat16 [65536, 2048], P('seq', 'head'), may hold values from -5 to 5
- lin_keys: bfloat16 [65536, 2048], P('seq', 'head'), may hold values from -6 to 6
- lin_values: bfloat16 [65536, 2048], P('seq', 'head'), may hold values from -6 to 6
- window_keys: bfloat16 [65536, 512], P('seq', 'head'), may hold values from -5 to 5
- window_values: bfloat16 [65536, 512], P('seq', 'head'), may hold values from -6 to 6
- level_index: int32 [17, 65536], P(None, 'seq'), may hold values from 0 to 7
- level_table: float32 [8, 16], P(None, 'head'), may hold values from 0.25 to 2
- seq_lengths: int32 [4], replicated, may hold values from 1 to 32, 64 in all
- gain_linear: float32 [2048], P('head'), may hold values from 0.25 to 1.75
- gain_window: float32 [2048], P('head'), may hold values from 0.25 to 1.75
- w_out: bfloat16 [2048, 2048], P('head'), may hold values from -0.125 to 0.125
Outputs:
- mixed: bfloat16 [65536, 2048], P(('seq', 'head'))
Inputs may be any that keep to these rules, and one draw needn't show every extreme that they name: `seq_lengths`: lengths of 4 consecutive sequences in whole shards of 1024 tokens, in order from token 0; they add up to the shards of seq and the longest has exactly half of them.
All inputs are finite; a program needn't handle non-finite values.
Results may differ from a plain program's by a relative error of at most 0.0095.
Values may be sent and summed in bfloat16 or wider, within the bound.
A program may use at most 128 MiB of HBM per device.

v0:
```python
import jax
import jax.numpy as jnp
from jax import lax
from jax.sharding import PartitionSpec as P

DH = 128
WINDOW = 256
BLOCK = 512


PRECISE = lax.Precision.HIGHEST
EPSILON = 1e-06


def passed_along(block, axis, distance):
    devices = range(lax.axis_size(axis))
    route = [(i - distance, i) for i in devices if i - distance in devices]
    return lax.ppermute(block, axis, route)


def swapped(block, axis, bit):
    count = lax.axis_size(axis)
    route = []
    for low in range(count):
        high = low | 1 << bit
        if high != low and high < count:
            route += [(low, high), (high, low)]
    return lax.ppermute(block, axis, route)


def bit_count(values, bit_width):
    running_total = jnp.zeros_like(values)
    for shift_by in range(bit_width):
        running_total = running_total + (values >= 1 << shift_by).astype(values.dtype)
    return running_total


def rms_scale(values, gain_vector):
    mean_square = jnp.mean(values * values, axis=-1, keepdims=True)
    return values * lax.rsqrt(mean_square + EPSILON) * gain_vector


def shards(
    queries,
    lin_keys,
    lin_values,
    window_keys,
    window_values,
    level_index,
    level_table,
    seq_lengths,
    gain_linear,
    gain_window,
    w_out,
):
    local_tokens = queries.shape[0]
    local_heads = level_table.shape[1]
    local_groups = window_keys.shape[1] // DH
    members = local_heads // local_groups
    level_total = level_index.shape[0]
    block_bits = BLOCK.bit_length() - 1
    local_blocks = local_tokens // BLOCK
    shard_bits = lax.axis_size("seq").bit_length() - 1
    shard_id = lax.axis_index("seq")
    seq_ends = jnp.cumsum(seq_lengths)
    seq_starts = seq_ends - seq_lengths
    seq_begin = jnp.max(jnp.where(seq_starts <= shard_id, seq_starts, 0))
    opens_here = seq_begin == shard_id
    table_rows = jnp.arange(level_table.shape[0], dtype=jnp.int32)
    one_hot = (level_index[:, :, None] == table_rows[None, None, :]).astype(jnp.float32)
    level_scale = jnp.exp2(-0.5 * jnp.arange(level_total, dtype=jnp.float32))
    weights = (
        jnp.einsum("ltk,kh->lth", one_hot, level_table, precision=PRECISE)
        * level_scale[:, None, None]
    )
    query_heads = queries.reshape(local_tokens, local_heads, DH)
    key_heads = lin_keys.reshape(local_tokens, local_heads, DH)
    value_heads = lin_values.reshape(local_tokens, local_heads, DH)
    window_key_heads = window_keys.reshape(local_tokens, local_groups, DH)
    window_value_heads = window_values.reshape(local_tokens, local_groups, DH)
    rim_keys, rim_values = passed_along(
        (window_key_heads[local_tokens - WINDOW :], window_value_heads[local_tokens - WINDOW :]),
        "seq",
        1,
    )
    block_states = jnp.einsum(
        "cshd,cshe->chde",
        key_heads.reshape(local_blocks, BLOCK, local_heads, DH),
        value_heads.reshape(local_blocks, BLOCK, local_heads, DH),
        preferred_element_type=jnp.float32,
    )
    shard_state = jnp.sum(block_states, axis=0)
    running = shard_state
    opened = opens_here.astype(jnp.float32).reshape(1)
    collected = []
    for bit_number in range(shard_bits):
        partner_sum, partner_open = (
            swapped(running.astype(jnp.bfloat16), "seq", bit_number).astype(running.dtype),
            swapped(opened.astype(jnp.bfloat16), "seq", bit_number).astype(opened.dtype),
        )
        group_span = 1 << bit_number
        upper_half = shard_id // group_span % 2 == 1
        reaches = seq_begin < shard_id // group_span * group_span
        collected.append(jnp.where(upper_half & reaches, partner_sum, 0.0))
        running = jnp.where(
            upper_half,
            running + (1.0 - opened) * partner_sum,
            partner_sum + (1.0 - partner_open) * running,
        )
        opened = jnp.maximum(opened, partner_open)
    shard_levels = jnp.stack(collected)
    extended_keys = jnp.concatenate([rim_keys, window_key_heads], axis=0)
    extended_values = jnp.concatenate([rim_values, window_value_heads], axis=0)
    offsets = jnp.arange(BLOCK, dtype=jnp.int32)
    level_grid = bit_count(jnp.bitwise_xor(offsets[:, None], offsets[None, :]), block_bits)
    causal = offsets[None, :] <= offsets[:, None]
    window_offsets = jnp.arange(BLOCK + WINDOW, dtype=jnp.int32) - WINDOW
    linear_gain = gain_linear.reshape(local_heads, DH)
    window_gain = gain_window.reshape(local_heads, DH)
    zero_state = jnp.zeros((local_heads, DH, DH), jnp.float32)
    outputs = []
    for block_id in range(local_blocks):
        first_row = block_id * BLOCK
        query_block = query_heads[first_row : first_row + BLOCK]
        key_block = key_heads[first_row : first_row + BLOCK]
        value_block = value_heads[first_row : first_row + BLOCK]
        weight_block = weights[:, first_row : first_row + BLOCK]
        scores = jnp.einsum(
            "thd,shd->hts", query_block, key_block, preferred_element_type=jnp.float32
        )
        mixing = jnp.zeros((local_heads, BLOCK, BLOCK), jnp.float32)
        for level_id in range(block_bits + 1):
            mixing = (
                mixing
                + jnp.where(level_grid == level_id, 1.0, 0.0)[None, :, :]
                * weight_block[level_id].T[:, :, None]
            )
        mixing = jnp.where(causal[None, :, :], mixing, 0.0)
        near_part = jnp.einsum(
            "hts,shd->thd",
            (scores * mixing).astype(jnp.bfloat16),
            value_block,
            preferred_element_type=jnp.float32,
        )
        local_levels = []
        bit_number = 0
        group_span = 1 << bit_number
        upper_edge = block_id // group_span * group_span
        if block_id // group_span % 2 == 1:
            local_levels.append(jnp.sum(block_states[upper_edge - group_span : upper_edge], axis=0))
        else:
            local_levels.append(zero_state)
        states_stack = jnp.concatenate([jnp.stack(local_levels), shard_levels], axis=0)
        far_weights = weight_block[block_bits + 1 :]
        query_float = query_block.astype(jnp.float32)
        far_part = jnp.zeros((BLOCK, local_heads, DH), jnp.float32)
        for level_id in range(states_stack.shape[0]):
            reached = jnp.einsum(
                "thd,hde->the", query_float, states_stack[level_id], precision=PRECISE
            )
            far_part = far_part + far_weights[level_id][:, :, None] * reached
        linear_part = rms_scale(near_part + far_part, linear_gain)
        key_window = extended_keys[first_row : first_row + BLOCK + WINDOW]
        value_window = extended_values[first_row : first_row + BLOCK + WINDOW]
        key_pos = first_row + window_offsets
        query_pos = first_row + offsets
        allowed = (
            (key_pos[None, :] <= query_pos[:, None])
            & (key_pos[None, :] > query_pos[:, None] - WINDOW)
            & ((key_pos[None, :] >= 0) | jnp.logical_not(opens_here))
        )
        grouped = query_block.reshape(BLOCK, local_groups, members, DH)
        logits = jnp.einsum(
            "tkgd,skd->kgts", grouped, key_window, preferred_element_type=jnp.float32
        ) * DH ** (-0.5)
        logits = jnp.where(allowed[None, None, :, :], logits, -1e30)
        row_peak = jnp.max(logits, axis=-1, keepdims=True)
        exponents = jnp.exp(logits - row_peak)
        window_weights = (exponents / jnp.sum(exponents, axis=-1, keepdims=True)).astype(
            jnp.bfloat16
        )
        window_raw = jnp.einsum(
            "kgts,skd->tkgd", window_weights, value_window, preferred_element_type=jnp.float32
        ).reshape(BLOCK, local_heads, DH)
        window_part = rms_scale(window_raw, window_gain)
        outputs.append(
            (linear_part + window_part).astype(jnp.bfloat16).reshape(BLOCK, local_heads * DH)
        )
    attended = jnp.concatenate(outputs, axis=0)
    return lax.psum_scatter(
        jnp.dot(attended, w_out, preferred_element_type=jnp.float32).astype(jnp.bfloat16),
        "head",
        scatter_dimension=0,
        tiled=True,
    )


def solution(mesh):
    placed = (
        P("seq", "head"),
        P("seq", "head"),
        P("seq", "head"),
        P("seq", "head"),
        P("seq", "head"),
        P(None, "seq"),
        P(None, "head"),
        P(),
        P("head"),
        P("head"),
        P("head", None),
    )
    return jax.shard_map(
        shards, mesh=mesh, in_specs=placed, out_specs=P(("seq", "head"), None), check_vma=False
    )
```

profile of v0, /device:TPU:1, one launch (start us, length us, event | category | flops | bytes accessed | tf_op | source)
XLA Modules:
  0.0 240.1 jit_solution(17859323758520135967)
XLA Ops:
  6.5 0.8 reduce-window.9
  7.4 1.3 fusion.124
  9.3 2.9 %collective-permute-start.1 = (bf16[1]{0:T(256)(128)(2,1)}, bf16[1]{0:T(256)(128)(2,1)}, u32[]{:S(2)}, u32[]{:S(2)}) collective-permute-start(bf16[1]{0:T(256)(128)(2,1)} %convert_element_type.751), channel_id=1, source_target_pairs={{0,2},{2,0},{4,6},{6,4},{8,10},{10,8},{12,14},{14,12},{16,18},{18,... | collective-permute-start | bytes 14 | tf_op jit(solution)/shard_map/ppermute | solution.py:28
  12.3 2.4 copy.177
  15.3 2.2 fusion.161
  19.6 3.9 %collective-permute-start.12 = (bf16[256,2,128]{2,0,1:T(8,128)(2,1)}, bf16[256,2,128]{2,0,1:T(8,128)(2,1)}, u32[]{:S(2)}, u32[]{:S(2)}) collective-permute-start(bf16[256,2,128]{2,0,1:T(8,128)(2,1)} %copy.119), channel_id=1, source_target_pairs={{0,2},{2,4},{4,6},{6,8},{8,10},{10,12},{12,14},{14,16},{16,18},{18... | collective-permute-start | bytes 393224 | tf_op jit(solution)/shard_map/ppermute | solution.py:18
  23.6 3.7 %collective-permute-start.11 = (bf16[256,2,128]{0,2,1:T(8,128)(2,1)S(1)}, bf16[256,2,128]{0,2,1:T(8,128)(2,1)}, u32[]{:S(2)}, u32[]{:S(2)}) collective-permute-start(bf16[256,2,128]{0,2,1:T(8,128)(2,1)S(1)} %bitcast.380), channel_id=1, source_target_pairs={{0,2},{2,4},{4,6},{6,8},{8,10},{10,12},{12,14},{14,16},{16,18},{18... | collective-permute-start | bytes 393224 | tf_op jit(solution)/shard_map/ppermute | solution.py:18
  28.0 1.7 compare_select_fusion
  29.7 1.8 compare_select_fusion.2
  31.5 1.7 compare_select_fusion.4
  33.2 1.8 compare_select_fusion.6
  35.0 1.7 compare_select_fusion.8
  36.7 1.2 fusion.153
  38.7 1.5 fusion.154
  42.9 1.8 slice.266
  46.5 2.1 copy.117
  49.2 3.1 %fusion.155 = (bf16[512,1024]{1,0:T(8,128)(2,1)}, bf16[512,1024]{1,0:T(8,128)(2,1)}) fusion(bf16[1024,1024]{1,0:T(8,128)(2,1)} %param.11), kind=kLoop, calls=%fused_computation.254 | loop fusion | bytes 4194304 | tf_op jit(solution)/shard_map/slice | solution.py:124
  52.2 1.5 copy.175
  56.3 1.3 copy.176
  57.6 2.3 copy.128
  59.9 1.5 copy.173
  61.4 2.3 copy.174
  63.7 2.3 copy.103
  66.0 2.3 fusion.100
  68.3 1.9 copy.140
  70.2 1.2 and_and_fusion
  71.4 8.3 %fusion.162 = (f32[2,4,512]{2,1,0:T(4,128)S(1)}, f32[2,4,512,768]{2,3,1,0:T(8,128)}) fusion(pred[512,768]{0,1:T(8,128)(4,1)} %and_and_fusion, bf16[768,2,128,1]{0,2,3,1:T(8,128)(2,1)S(1)} %bitcast.368, bf16[512,2,4,128]{0,3,2,1:T(8,128)(2,1)S(1)} %bitcast.347), kind=kOutput, calls=%fused_computation.257 | convolution fusion | flops 817890048 | bytes 14434304 | tf_op jit(solution)/shard_map/sub | solution.py:178
  79.7 7.2 %fusion.27 = (f32[512,2,4]{0,2,1:T(4,128)S(1)}, f32[2,4,512,128]{2,3,1,0:T(8,128)}) fusion(bf16[768,2,128,1]{0,2,3,1:T(8,128)(2,1)} %bitcast.379, f32[2,4,512,768]{2,3,1,0:T(8,128)} %get-tuple-element.58, f32[2,4,512]{2,1,0:T(4,128)S(1)} %get-tuple-element.57), kind=kOutput, calls=%fused_computation.37 | convolution fusion | flops 812642304 | bytes 15106048 | tf_op jit(solution)/shard_map/kgts,skd->tkgd/dot_general | solution.py:182
  88.3 1.0 copy.121
  89.4 3.5 %fusion.82 = f32[8,128,512]{2,1,0:T(8,128)} fusion(bf16[512,8,128]{0,2,1:T(8,128)(2,1)S(1)} %bitcast.348, f32[2,8,128,128]{3,2,1,0:T(8,128)} %get-tuple-element.52), kind=kOutput, calls=%fused_computation.140 | convolution fusion | flops 805306368 | bytes 3670016 | tf_op jit(solution)/shard_map/thd,hde->the/dot_general | solution.py:158
  93.0 13.2 %fusion.13 = f32[8,512,128]{1,2,0:T(8,128)} fusion(bf16[512,8,128]{0,2,1:T(8,128)(2,1)} %bitcast.376, f32[8,512]{1,0:T(8,128)S(1)} %copy-done.42, f32[8,512]{1,0:T(8,128)S(1)} %copy-done.43, f32[8,512]{1,0:T(8,128)S(1)} %copy-done.44, f32[8,512]{1,0:T(8,128)S(1)} %copy-done.45, f32[8,512]{1,0:T(8,128)S(1)} %copy-done.46, f32[8,512]{1,0:T(8,128)} %get-tuple-element.26, ...), kind=kOutput, calls=%fused_computation.21 | convolution fusion | flops 1119879168 | bytes 16154624 | tf_op jit(solution)/shard_map/hts,shd->thd/dot_general | solution.py:139
  106.3 13.6 %fusion.12 = f32[8,512,128]{1,2,0:T(8,128)} fusion(bf16[512,8,128]{0,2,1:T(8,128)(2,1)} %bitcast.374, f32[8,512]{1,0:T(8,128)S(1)} %copy-done.32, f32[512,512]{1,0:T(8,128)} %get-tuple-element.63, f32[8,512]{1,0:T(8,128)S(1)} %copy-done.33, f32[512,512]{1,0:T(8,128)} %get-tuple-element.64, f32[8,512]{1,0:T(8,128)S(1)} %copy-done.34, ...), kind=kOutput, calls=%fused_computation.20 | convolution fusion | flops 1119879168 | bytes 16154624 | tf_op jit(solution)/shard_map/hts,shd->thd/dot_general | solution.py:139
  120.0 1.2 fusion.47
  121.8 2.8 %collective-permute-start.3 = (bf16[1]{0:T(256)(128)(2,1)}, bf16[1]{0:T(256)(128)(2,1)}, u32[]{:S(2)}, u32[]{:S(2)}) collective-permute-start(bf16[1]{0:T(256)(128)(2,1)} %convert_element_type.755), channel_id=1, source_target_pairs={{0,4},{4,0},{2,6},{6,2},{8,12},{12,8},{10,14},{14,10},{16,20},{20,... | collective-permute-start | bytes 14 | tf_op jit(solution)/shard_map/ppermute | solution.py:28
  126.6 1.8 collective-permute-start.5
  129.8 4.0 %collective-permute-start.7 = (bf16[1]{0:T(256)(128)(2,1)}, bf16[1]{0:T(256)(128)(2,1)}, u32[]{:S(2)}, u32[]{:S(2)}) collective-permute-start(bf16[1]{0:T(256)(128)(2,1)} %convert_element_type.763), channel_id=1, source_target_pairs={{0,16},{16,0},{2,18},{18,2},{4,20},{20,4},{6,22},{22,6},{8,24},{24... | collective-permute-start | bytes 14 | tf_op jit(solution)/shard_map/ppermute | solution.py:28
  135.1 2.4 %collective-permute-start.9 = (bf16[1]{0:T(256)(128)(2,1)}, bf16[1]{0:T(256)(128)(2,1)}, u32[]{:S(2)}, u32[]{:S(2)}) collective-permute-start(bf16[1]{0:T(256)(128)(2,1)} %convert_element_type.767), channel_id=1, source_target_pairs={{0,32},{32,0},{2,34},{34,2},{4,36},{36,4},{6,38},{38,6},{8,40},{40... | collective-permute-start | bytes 14 | tf_op jit(solution)/shard_map/ppermute | solution.py:28
  138.7 10.9 %fusion.156 = (f32[2,4,512]{2,1,0:T(4,128)}, f32[2,4,512,768]{2,3,1,0:T(8,128)}) fusion(pred[512,768]{0,1:T(8,128)(4,1)} %fusion.47, bf16[512,2,4,128]{0,3,2,1:T(8,128)(2,1)S(1)} %bitcast.358, bf16[1024,2,128]{2,0,1:T(8,128)(2,1)} %copy.121, bf16[256,2,128]{2,0,1:T(8,128)(2,1)} %collective-permute-done.12), kind=kOutput, calls=%fused_computation.255 | convolution fusion | flops 818676480 | bytes 14696448 | tf_op jit(solution)/shard_map/sub | solution.py:178
  149.6 7.1 %fusion.35 = (f32[512,2,4]{0,2,1:T(4,128)S(1)}, f32[2,128,4,512]{3,1,2,0:T(8,128)}) fusion(f32[2,4,512,768]{2,3,1,0:T(8,128)} %get-tuple-element.50, f32[2,4,512]{2,1,0:T(4,128)} %get-tuple-element.49, bf16[1024,2,128]{0,2,1:T(8,128)(2,1)S(1)} %bitcast.377, bf16[256,2,128]{0,2,1:T(8,128)(2,1)} %collective-permute-done.11), kind=kOutput, calls=%fused_computation.53 | convolution fusion | flops 813428736 | bytes 15368192 | tf_op jit(solution)/shard_map/kgts,skd->tkgd/dot_general | solution.py:182
  156.9 2.1 collective-permute-start.2
  159.0 1.0 fusion.61
  160.0 1.0 fusion.62
  161.0 2.6 %collective-permute-done.2 = bf16[8,128,128]{1,2,0:T(8,128)(2,1)S(1)} collective-permute-done((bf16[8,128,128]{1,2,0:T(8,128)(2,1)S(1)}, bf16[8,128,128]{1,2,0:T(8,128)(2,1)S(1)}, u32[]{:S(2)}, u32[]{:S(2)}) %collective-permute-start.2) | collective-permute-done | bytes 262176 | tf_op jit(solution)/shard_map/ppermute | solution.py:28
  164.4 1.0 fusion.63
  165.5 1.0 fusion.64
  166.5 3.0 %collective-permute-done.4 = bf16[8,128,128]{1,2,0:T(8,128)(2,1)S(1)} collective-permute-done((bf16[8,128,128]{1,2,0:T(8,128)(2,1)S(1)}, bf16[8,128,128]{1,2,0:T(8,128)(2,1)S(1)}, u32[]{:S(2)}, u32[]{:S(2)}) %collective-permute-start.4) | collective-permute-done | bytes 262176 | tf_op jit(solution)/shard_map/ppermute | solution.py:28
  169.8 2.7 %collective-permute-start.6 = (bf16[8,128,128]{1,2,0:T(8,128)(2,1)S(1)}, bf16[8,128,128]{1,2,0:T(8,128)(2,1)S(1)}, u32[]{:S(2)}, u32[]{:S(2)}) collective-permute-start(bf16[8,128,128]{1,2,0:T(8,128)(2,1)S(1)} %get-tuple-element.5), channel_id=1, source_target_pairs={{0,16},{16,0},{2,18},{18,2},{4,20},{20,4},{6,22},{22,6},{8,24},{24... | collective-permute-start | bytes 786440 | tf_op jit(solution)/shard_map/ppermute | solution.py:28
  172.6 1.0 fusion.65
  173.6 1.0 fusion.66
  174.6 4.0 %collective-permute-done.6 = bf16[8,128,128]{1,2,0:T(8,128)(2,1)S(1)} collective-permute-done((bf16[8,128,128]{1,2,0:T(8,128)(2,1)S(1)}, bf16[8,128,128]{1,2,0:T(8,128)(2,1)S(1)}, u32[]{:S(2)}, u32[]{:S(2)}) %collective-permute-start.6) | collective-permute-done | bytes 262176 | tf_op jit(solution)/shard_map/ppermute | solution.py:28
  178.7 1.0 collective-permute-start.8
  179.7 1.0 fusion.67
  180.7 1.0 fusion.68
  181.7 2.3 collective-permute-done.8
  184.3 2.5 %collective-permute-start.10 = (bf16[8,128,128]{1,2,0:T(8,128)(2,1)S(1)}, bf16[8,128,128]{1,2,0:T(8,128)(2,1)S(1)}, u32[]{:S(2)}, u32[]{:S(2)}) collective-permute-start(bf16[8,128,128]{1,2,0:T(8,128)(2,1)S(1)} %fusion.81), channel_id=1, source_target_pairs={{0,64},{64,0},{2,66},{66,2},{4,68},{68,4},{6,70},{70,6},{8,72},{72... | collective-permute-start | bytes 786440 | tf_op jit(solution)/shard_map/ppermute | solution.py:28
  186.8 1.0 fusion.69
  187.9 1.0 fusion.70
  188.9 2.2 collective-permute-done.10
  191.2 3.4 %multiply_reduce_fusion = (f32[512,8]{0,1:T(8,128)S(1)}, f32[512,8,128]{0,2,1:T(8,128)S(1)}) fusion(bf16[512,8,128]{0,2,1:T(8,128)(2,1)S(1)} %bitcast.355, bf16[8,128,128]{1,2,0:T(8,128)(2,1)S(1)} %collective-permute-done.10, pred[]{:T(512)S(6)} %and.127, f32[512,8]{0,1:T(8,128)S(1)} %copy-done.24, f32[8,128,512]{2,1,0:T(8,128)S(1)} %fusion.69, ...), kind=kOutput, calls=%fused_computation.71 | convolution fusion | flops 813953024 | bytes 18219008 | tf_op jit(solution)/shard_map/thd,hde->the/dot_general | solution.py:158
  194.7 3.4 %multiply_reduce_fusion.1 = (f32[512,8]{0,1:T(8,128)S(1)}, f32[512,8,128]{0,2,1:T(8,128)S(1)}) fusion(bf16[512,8,128]{0,2,1:T(8,128)(2,1)S(1)} %bitcast.364, bf16[8,128,128]{1,2,0:T(8,128)(2,1)S(1)} %collective-permute-done.10, pred[]{:T(512)S(6)} %and.127, f32[512,8]{0,1:T(8,128)S(1)} %copy-done.18, f32[8,128,512]{2,1,0:T(8,128)S(1)} %fusion.70, ...), kind=kOutput, calls=%fused_computation.72 | convolution fusion | flops 813953024 | bytes 18219008 | tf_op jit(solution)/shard_map/thd,hde->the/dot_general | solution.py:158
  198.2 1.1 fusion.26
  199.3 1.1 copy-done.51
  200.3 6.5 %convolution_convert_fusion = bf16[1024,2048]{1,0:T(8,128)(2,1)} fusion(bf16[1024,2048]{1,0:T(8,128)(2,1)S(1)} %copy-done.51, bf16[512,1024]{0,1:T(8,128)(2,1)S(1)} %bitcast.372, bf16[512,1024]{0,1:T(8,128)(2,1)S(1)} %bitcast.371), kind=kOutput, calls=%fused_computation.22 | convolution fusion | flops 4301258752 | bytes 10485760 | tf_op jit(solution)/shard_map/dot_general | solution.py:191
  206.8 26.2 %reduce-scatter.2.cloned.1.call-done = bf16[512,2048]{1,0:T(8,128)(2,1)} async-done(((bf16[1024,2048]{1,0:T(8,128)(2,1)}), bf16[512,2048]{1,0:T(8,128)(2,1)}) %reduce-scatter.2.cloned.1.call-update) | async-done | bytes 2097168 | tf_op jit(solution)/shard_map/reduce_scatter | solution.py:190
  (148 shorter events, 12.1 us)
Async XLA Ops:
  6.5 34.4 %copy-start = (f32[8,8]{1,0:T(8,128)S(1)}, f32[8,8]{1,0:T(8,128)}, u32[]{:S(2)}) copy-start(f32[8,8]{1,0:T(8,128)} %param.17) | copy-start | bytes 772
  6.5 226.5 %reduce-scatter.2.cloned.1.call-start = ((), (), s32[]{:S(2)}) async-start(), calls=%async_computation.1 | async-start | bytes 6291456 | tf_op jit(solution)/shard_map/reduce_scatter | solution.py:190
  9.3 111.8 %collective-permute-start.1 = (bf16[1]{0:T(256)(128)(2,1)}, bf16[1]{0:T(256)(128)(2,1)}, u32[]{:S(2)}, u32[]{:S(2)}) collective-permute-start(bf16[1]{0:T(256)(128)(2,1)} %convert_element_type.751), channel_id=1, source_target_pairs={{0,2},{2,0},{4,6},{6,4},{8,10},{10,8},{12,14},{14,12},{16,18},{18,... | collective-permute-start | bytes 14 | tf_op jit(solution)/shard_map/ppermute | solution.py:28
  12.3 2.4 copy-start.3
  17.4 6.1 %slice-start.1 = ((bf16[1024,256]{1,0:T(8,128)(2,1)}), bf16[256,256]{1,0:T(8,128)(2,1)S(1)}, s32[]{:S(2)}) async-start(bf16[1024,256]{1,0:T(8,128)(2,1)} %param.15), calls=%async_computation.3 | async-start | bytes 262144 | tf_op jit(solution)/shard_map/slice | solution.py:82
  18.4 138.3 %collective-permute-start = (bf16[8,128,128]{1,2,0:T(8,128)(2,1)}, bf16[8,128,128]{1,2,0:T(8,128)(2,1)S(1)}, u32[]{:S(2)}, u32[]{:S(2)}) collective-permute-start(bf16[8,128,128]{1,2,0:T(8,128)(2,1)} %convert_element_type.749), channel_id=1, source_target_pairs={{0,2},{2,0},{4,6},{6,4},{8,10},{10,8},{12,14},{14,12},{16,18},{18,... | collective-permute-start | bytes 786440 | tf_op jit(solution)/shard_map/ppermute | solution.py:28
  18.7 24.2 %copy-start.7 = (bf16[1024,256]{0,1:T(8,128)(2,1)}, bf16[1024,256]{0,1:T(8,128)(2,1)S(1)}, u32[]{:S(2)}) copy-start(bf16[1024,256]{0,1:T(8,128)(2,1)S(1)} %copy.118) | copy-start | bytes 1572868
  19.6 119.1 %collective-permute-start.12 = (bf16[256,2,128]{2,0,1:T(8,128)(2,1)}, bf16[256,2,128]{2,0,1:T(8,128)(2,1)}, u32[]{:S(2)}, u32[]{:S(2)}) collective-permute-start(bf16[256,2,128]{2,0,1:T(8,128)(2,1)} %copy.119), channel_id=1, source_target_pairs={{0,2},{2,4},{4,6},{6,8},{8,10},{10,12},{12,14},{14,16},{16,18},{18... | collective-permute-start | bytes 393224 | tf_op jit(solution)/shard_map/ppermute | solution.py:18
  23.6 126.0 %collective-permute-start.11 = (bf16[256,2,128]{0,2,1:T(8,128)(2,1)S(1)}, bf16[256,2,128]{0,2,1:T(8,128)(2,1)}, u32[]{:S(2)}, u32[]{:S(2)}) collective-permute-start(bf16[256,2,128]{0,2,1:T(8,128)(2,1)S(1)} %bitcast.380), channel_id=1, source_target_pairs={{0,2},{2,4},{4,6},{6,8},{8,10},{10,12},{12,14},{14,16},{16,18},{18... | collective-permute-start | bytes 393224 | tf_op jit(solution)/shard_map/ppermute | solution.py:18
  33.2 3.5 %copy-start.2 = (bf16[1024,1024]{1,0:T(8,128)(2,1)S(1)}, bf16[1024,1024]{1,0:T(8,128)(2,1)}, u32[]{:S(2)}) copy-start(bf16[1024,1024]{1,0:T(8,128)(2,1)} %param.12) | copy-start | bytes 6291460
  66.0 5.4 %slice-start = ((bf16[1024,256]{0,1:T(8,128)(2,1)}), bf16[768,256]{0,1:T(8,128)(2,1)S(1)}, s32[]{:S(2)}) async-start(bf16[1024,256]{0,1:T(8,128)(2,1)} %copy-done.7), calls=%async_computation.2 | async-start | bytes 786432 | tf_op jit(solution)/shard_map/slice | solution.py:163
  79.7 8.6 %copy-start.8 = (bf16[1024,256]{0,1:T(8,128)(2,1)S(1)}, bf16[1024,256]{0,1:T(8,128)(2,1)}, u32[]{:S(2)}) copy-start(bf16[1024,256]{0,1:T(8,128)(2,1)} %copy-done.7) | copy-start | bytes 1572868
  89.3 3.6 %copy-start.15 = (pred[512,512]{1,0:T(8,128)(4,1)S(1)}, pred[512,512]{1,0:T(8,128)(4,1)}, u32[]{:S(2)}) copy-start(pred[512,512]{1,0:T(8,128)(4,1)} %iota_compare_fusion.1) | copy-start | bytes 786436
  89.3 3.6 %copy-start.42 = (f32[8,512]{1,0:T(8,128)S(1)}, f32[8,512]{1,0:T(8,128)}, u32[]{:S(2)}) copy-start(f32[8,512]{1,0:T(8,128)} %get-tuple-element.21) | copy-start | bytes 49156
  89.3 3.6 %copy-start.43 = (f32[8,512]{1,0:T(8,128)S(1)}, f32[8,512]{1,0:T(8,128)}, u32[]{:S(2)}) copy-start(f32[8,512]{1,0:T(8,128)} %get-tuple-element.22) | copy-start | bytes 49156
  89.3 3.6 %copy-start.44 = (f32[8,512]{1,0:T(8,128)S(1)}, f32[8,512]{1,0:T(8,128)}, u32[]{:S(2)}) copy-start(f32[8,512]{1,0:T(8,128)} %get-tuple-element.23) | copy-start | bytes 49156
  89.3 3.6 %copy-start.45 = (f32[8,512]{1,0:T(8,128)S(1)}, f32[8,512]{1,0:T(8,128)}, u32[]{:S(2)}) copy-start(f32[8,512]{1,0:T(8,128)} %get-tuple-element.24) | copy-start | bytes 49156
  89.3 3.6 %copy-start.46 = (f32[8,512]{1,0:T(8,128)S(1)}, f32[8,512]{1,0:T(8,128)}, u32[]{:S(2)}) copy-start(f32[8,512]{1,0:T(8,128)} %get-tuple-element.25) | copy-start | bytes 49156
  92.9 13.3 %copy-start.32 = (f32[8,512]{1,0:T(8,128)S(1)}, f32[8,512]{1,0:T(8,128)}, u32[]{:S(2)}) copy-start(f32[8,512]{1,0:T(8,128)} %get-tuple-element.37) | copy-start | bytes 49156
  92.9 13.3 %copy-start.33 = (f32[8,512]{1,0:T(8,128)S(1)}, f32[8,512]{1,0:T(8,128)}, u32[]{:S(2)}) copy-start(f32[8,512]{1,0:T(8,128)} %get-tuple-element.38) | copy-start | bytes 49156
  92.9 13.3 %copy-start.34 = (f32[8,512]{1,0:T(8,128)S(1)}, f32[8,512]{1,0:T(8,128)}, u32[]{:S(2)}) copy-start(f32[8,512]{1,0:T(8,128)} %get-tuple-element.39) | copy-start | bytes 49156
  92.9 13.3 %copy-start.35 = (f32[8,512]{1,0:T(8,128)S(1)}, f32[8,512]{1,0:T(8,128)}, u32[]{:S(2)}) copy-start(f32[8,512]{1,0:T(8,128)} %get-tuple-element.40) | copy-start | bytes 49156
  92.9 13.3 %copy-start.36 = (f32[8,512]{1,0:T(8,128)S(1)}, f32[8,512]{1,0:T(8,128)}, u32[]{:S(2)}) copy-start(f32[8,512]{1,0:T(8,128)} %get-tuple-element.41) | copy-start | bytes 49156
  93.0 13.3 %copy-start.37 = (f32[8,512]{1,0:T(8,128)S(1)}, f32[8,512]{1,0:T(8,128)}, u32[]{:S(2)}) copy-start(f32[8,512]{1,0:T(8,128)} %get-tuple-element.42) | copy-start | bytes 49156
  93.0 13.3 %copy-start.38 = (f32[8,512]{1,0:T(8,128)S(1)}, f32[8,512]{1,0:T(8,128)}, u32[]{:S(2)}) copy-start(f32[8,512]{1,0:T(8,128)} %get-tuple-element.43) | copy-start | bytes 49156
  93.0 13.3 %copy-start.39 = (f32[8,512]{1,0:T(8,128)S(1)}, f32[8,512]{1,0:T(8,128)}, u32[]{:S(2)}) copy-start(f32[8,512]{1,0:T(8,128)} %get-tuple-element.44) | copy-start | bytes 49156
  93.0 13.3 %copy-start.40 = (f32[8,512]{1,0:T(8,128)S(1)}, f32[8,512]{1,0:T(8,128)}, u32[]{:S(2)}) copy-start(f32[8,512]{1,0:T(8,128)} %get-tuple-element.45) | copy-start | bytes 49156
  93.0 13.3 %copy-start.41 = (f32[8,512]{1,0:T(8,128)S(1)}, f32[8,512]{1,0:T(8,128)}, u32[]{:S(2)}) copy-start(f32[8,512]{1,0:T(8,128)} %get-tuple-element.46) | copy-start | bytes 49156
  106.3 13.7 %copy-start.31 = (s32[768]{0:T(1024)S(1)}, s32[768]{0:T(1024)}, u32[]{:S(2)}) copy-start(s32[768]{0:T(1024)} %iota_add_fusion.1) | copy-start | bytes 9220
  106.3 13.7 %copy-start.47 = (s32[512]{0:T(512)S(1)}, s32[512]{0:T(512)}, u32[]{:S(2)}) copy-start(s32[512]{0:T(512)} %iota_add_fusion.4) | copy-start | bytes 6148
  106.3 13.7 %copy-start.50 = (pred[768]{0:T(1024)(128)(4,1)S(1)}, pred[768]{0:T(1024)(128)(4,1)}, u32[]{:S(2)}) copy-start(pred[768]{0:T(1024)(128)(4,1)} %compare_or_fusion.1) | copy-start | bytes 2308
  121.8 4.1 %collective-permute-start.3 = (bf16[1]{0:T(256)(128)(2,1)}, bf16[1]{0:T(256)(128)(2,1)}, u32[]{:S(2)}, u32[]{:S(2)}) collective-permute-start(bf16[1]{0:T(256)(128)(2,1)} %convert_element_type.755), channel_id=1, source_target_pairs={{0,4},{4,0},{2,6},{6,2},{8,12},{12,8},{10,14},{14,10},{16,20},{20,... | collective-permute-start | bytes 14 | tf_op jit(solution)/shard_map/ppermute | solution.py:28
  126.6 2.6 %collective-permute-start.5 = (bf16[1]{0:T(256)(128)(2,1)}, bf16[1]{0:T(256)(128)(2,1)}, u32[]{:S(2)}, u32[]{:S(2)}) collective-permute-start(bf16[1]{0:T(256)(128)(2,1)} %convert_element_type.759), channel_id=1, source_target_pairs={{0,8},{8,0},{2,10},{10,2},{4,12},{12,4},{6,14},{14,6},{16,24},{24,... | collective-permute-start | bytes 14 | tf_op jit(solution)/shard_map/ppermute | solution.py:28
  129.8 4.7 %collective-permute-start.7 = (bf16[1]{0:T(256)(128)(2,1)}, bf16[1]{0:T(256)(128)(2,1)}, u32[]{:S(2)}, u32[]{:S(2)}) collective-permute-start(bf16[1]{0:T(256)(128)(2,1)} %convert_element_type.763), channel_id=1, source_target_pairs={{0,16},{16,0},{2,18},{18,2},{4,20},{20,4},{6,22},{22,6},{8,24},{24... | collective-permute-start | bytes 14 | tf_op jit(solution)/shard_map/ppermute | solution.py:28
  135.1 3.0 %collective-permute-start.9 = (bf16[1]{0:T(256)(128)(2,1)}, bf16[1]{0:T(256)(128)(2,1)}, u32[]{:S(2)}, u32[]{:S(2)}) collective-permute-start(bf16[1]{0:T(256)(128)(2,1)} %convert_element_type.767), channel_id=1, source_target_pairs={{0,32},{32,0},{2,34},{34,2},{4,36},{36,4},{6,38},{38,6},{8,40},{40... | collective-permute-start | bytes 14 | tf_op jit(solution)/shard_map/ppermute | solution.py:28
  138.7 10.9 %copy-start.14 = (bf16[1024,256]{0,1:T(8,128)(2,1)S(1)}, bf16[1024,256]{0,1:T(8,128)(2,1)}, u32[]{:S(2)}) copy-start(bf16[1024,256]{0,1:T(8,128)(2,1)} %copy.117) | copy-start | bytes 1572868
  156.9 6.8 %collective-permute-start.2 = (bf16[8,128,128]{1,2,0:T(8,128)(2,1)S(1)}, bf16[8,128,128]{1,2,0:T(8,128)(2,1)S(1)}, u32[]{:S(2)}, u32[]{:S(2)}) collective-permute-start(bf16[8,128,128]{1,2,0:T(8,128)(2,1)S(1)} %fusion.150), channel_id=1, source_target_pairs={{0,4},{4,0},{2,6},{6,2},{8,12},{12,8},{10,14},{14,10},{16,20},{20,... | collective-permute-start | bytes 786440 | tf_op jit(solution)/shard_map/ppermute | solution.py:28
  163.9 5.6 %collective-permute-start.4 = (bf16[8,128,128]{1,2,0:T(8,128)(2,1)S(1)}, bf16[8,128,128]{1,2,0:T(8,128)(2,1)S(1)}, u32[]{:S(2)}, u32[]{:S(2)}) collective-permute-start(bf16[8,128,128]{1,2,0:T(8,128)(2,1)S(1)} %fusion.115), channel_id=1, source_target_pairs={{0,8},{8,0},{2,10},{10,2},{4,12},{12,4},{6,14},{14,6},{16,24},{24,... | collective-permute-start | bytes 786440 | tf_op jit(solution)/shard_map/ppermute | solution.py:28
  169.8 8.8 %collective-permute-start.6 = (bf16[8,128,128]{1,2,0:T(8,128)(2,1)S(1)}, bf16[8,128,128]{1,2,0:T(8,128)(2,1)S(1)}, u32[]{:S(2)}, u32[]{:S(2)}) collective-permute-start(bf16[8,128,128]{1,2,0:T(8,128)(2,1)S(1)} %get-tuple-element.5), channel_id=1, source_target_pairs={{0,16},{16,0},{2,18},{18,2},{4,20},{20,4},{6,22},{22,6},{8,24},{24... | collective-permute-start | bytes 786440 | tf_op jit(solution)/shard_map/ppermute | solution.py:28
  178.7 5.3 %collective-permute-start.8 = (bf16[8,128,128]{1,2,0:T(8,128)(2,1)S(1)}, bf16[8,128,128]{1,2,0:T(8,128)(2,1)S(1)}, u32[]{:S(2)}, u32[]{:S(2)}) collective-permute-start(bf16[8,128,128]{1,2,0:T(8,128)(2,1)S(1)} %fusion.114), channel_id=1, source_target_pairs={{0,32},{32,0},{2,34},{34,2},{4,36},{36,4},{6,38},{38,6},{8,40},{40... | collective-permute-start | bytes 786440 | tf_op jit(solution)/shard_map/ppermute | solution.py:28
  184.3 6.8 %collective-permute-start.10 = (bf16[8,128,128]{1,2,0:T(8,128)(2,1)S(1)}, bf16[8,128,128]{1,2,0:T(8,128)(2,1)S(1)}, u32[]{:S(2)}, u32[]{:S(2)}) collective-permute-start(bf16[8,128,128]{1,2,0:T(8,128)(2,1)S(1)} %fusion.81), channel_id=1, source_target_pairs={{0,64},{64,0},{2,66},{66,2},{4,68},{68,4},{6,70},{70,6},{8,72},{72... | collective-permute-start | bytes 786440 | tf_op jit(solution)/shard_map/ppermute | solution.py:28
  186.8 4.3 %copy-start.12 = (f32[8,512,128]{1,2,0:T(8,128)S(1)}, f32[8,512,128]{1,2,0:T(8,128)}, u32[]{:S(2)}) copy-start(f32[8,512,128]{1,2,0:T(8,128)} %fusion.13) | copy-start | bytes 6291460
  187.8 3.3 %copy-start.5 = (f32[8,128,512]{2,1,0:T(8,128)S(1)}, f32[8,128,512]{2,1,0:T(8,128)}, u32[]{:S(2)}) copy-start(f32[8,128,512]{2,1,0:T(8,128)} %fusion.82) | copy-start | bytes 6291460
  187.8 3.3 %copy-start.24 = (f32[512,8]{0,1:T(8,128)S(1)}, f32[512,8]{0,1:T(8,128)}, u32[]{:S(2)}) copy-start(f32[512,8]{0,1:T(8,128)} %get-tuple-element.14) | copy-start | bytes 49156
  187.8 3.3 %copy-start.25 = (f32[512,8]{0,1:T(8,128)S(1)}, f32[512,8]{0,1:T(8,128)}, u32[]{:S(2)}) copy-start(f32[512,8]{0,1:T(8,128)} %get-tuple-element.15) | copy-start | bytes 49156
  187.8 3.3 %copy-start.26 = (f32[512,8]{0,1:T(8,128)S(1)}, f32[512,8]{0,1:T(8,128)}, u32[]{:S(2)}) copy-start(f32[512,8]{0,1:T(8,128)} %get-tuple-element.16) | copy-start | bytes 49156
  187.8 3.3 %copy-start.27 = (f32[512,8]{0,1:T(8,128)S(1)}, f32[512,8]{0,1:T(8,128)}, u32[]{:S(2)}) copy-start(f32[512,8]{0,1:T(8,128)} %get-tuple-element.17) | copy-start | bytes 49156
  187.8 3.3 %copy-start.28 = (f32[512,8]{0,1:T(8,128)S(1)}, f32[512,8]{0,1:T(8,128)}, u32[]{:S(2)}) copy-start(f32[512,8]{0,1:T(8,128)} %get-tuple-element.18) | copy-start | bytes 49156
  187.8 3.3 %copy-start.29 = (f32[512,8]{0,1:T(8,128)S(1)}, f32[512,8]{0,1:T(8,128)}, u32[]{:S(2)}) copy-start(f32[512,8]{0,1:T(8,128)} %get-tuple-element.19) | copy-start | bytes 49156
  187.8 3.3 %copy-start.30 = (f32[512,8]{0,1:T(8,128)S(1)}, f32[512,8]{0,1:T(8,128)}, u32[]{:S(2)}) copy-start(f32[512,8]{0,1:T(8,128)} %get-tuple-element.20) | copy-start | bytes 49156
  191.1 3.5 %copy-start.6 = (f32[8,128,512]{2,1,0:T(8,128)S(1)}, f32[8,128,512]{2,1,0:T(8,128)}, u32[]{:S(2)}) copy-start(f32[8,128,512]{2,1,0:T(8,128)} %fusion.100) | copy-start | bytes 6291460
  191.1 3.5 %copy-start.11 = (f32[8,512,128]{1,2,0:T(8,128)S(1)}, f32[8,512,128]{1,2,0:T(8,128)}, u32[]{:S(2)}) copy-start(f32[8,512,128]{1,2,0:T(8,128)} %fusion.12) | copy-start | bytes 6291460
  191.2 3.5 %copy-start.17 = (f32[512,8]{0,1:T(8,128)S(1)}, f32[512,8]{0,1:T(8,128)}, u32[]{:S(2)}) copy-start(f32[512,8]{0,1:T(8,128)} %get-tuple-element.13) | copy-start | bytes 49156
  191.2 3.5 %copy-start.18 = (f32[512,8]{0,1:T(8,128)S(1)}, f32[512,8]{0,1:T(8,128)}, u32[]{:S(2)}) copy-start(f32[512,8]{0,1:T(8,128)} %get-tuple-element.31) | copy-start | bytes 49156
  191.2 3.5 %copy-start.19 = (f32[512,8]{0,1:T(8,128)S(1)}, f32[512,8]{0,1:T(8,128)}, u32[]{:S(2)}) copy-start(f32[512,8]{0,1:T(8,128)} %get-tuple-element.32) | copy-start | bytes 49156
  191.2 3.5 %copy-start.20 = (f32[512,8]{0,1:T(8,128)S(1)}, f32[512,8]{0,1:T(8,128)}, u32[]{:S(2)}) copy-start(f32[512,8]{0,1:T(8,128)} %get-tuple-element.33) | copy-start | bytes 49156
  191.2 3.5 %copy-start.21 = (f32[512,8]{0,1:T(8,128)S(1)}, f32[512,8]{0,1:T(8,128)}, u32[]{:S(2)}) copy-start(f32[512,8]{0,1:T(8,128)} %get-tuple-element.34) | copy-start | bytes 49156
  191.2 3.5 %copy-start.22 = (f32[512,8]{0,1:T(8,128)S(1)}, f32[512,8]{0,1:T(8,128)}, u32[]{:S(2)}) copy-start(f32[512,8]{0,1:T(8,128)} %get-tuple-element.35) | copy-start | bytes 49156
  191.2 3.5 %copy-start.23 = (f32[512,8]{0,1:T(8,128)S(1)}, f32[512,8]{0,1:T(8,128)}, u32[]{:S(2)}) copy-start(f32[512,8]{0,1:T(8,128)} %get-tuple-element.36) | copy-start | bytes 49156
  194.7 3.4 %copy-start.9 = (f32[2,4,512,128]{2,3,1,0:T(8,128)S(1)}, f32[2,4,512,128]{2,3,1,0:T(8,128)}, u32[]{:S(2)}) copy-start(f32[2,4,512,128]{2,3,1,0:T(8,128)} %get-tuple-element.60) | copy-start | bytes 6291460
  194.7 3.4 %copy-start.10 = (f32[2,128,4,512]{3,1,2,0:T(8,128)S(1)}, f32[2,128,4,512]{3,1,2,0:T(8,128)}, u32[]{:S(2)}) copy-start(f32[2,128,4,512]{3,1,2,0:T(8,128)} %get-tuple-element.54) | copy-start | bytes 6291460
  194.7 3.4 %copy-start.48 = (f32[1024]{0:T(1024)S(1)}, f32[1024]{0:T(1024)}, u32[]{:S(2)}) copy-start(f32[1024]{0:T(1024)} %param.20) | copy-start | bytes 12292
  194.7 3.4 %copy-start.49 = (f32[1024]{0:T(1024)S(1)}, f32[1024]{0:T(1024)}, u32[]{:S(2)}) copy-start(f32[1024]{0:T(1024)} %param.19) | copy-start | bytes 12292
  206.8 26.2 %copy-start.1 = (f32[8,8]{1,0:T(8,128)S(1)}, f32[8,8]{1,0:T(8,128)}, u32[]{:S(2)}) copy-start(f32[8,8]{1,0:T(8,128)} %param.17) | copy-start | bytes 772
  (4 other events, 7.5 us)
Sparse Core Ops, SparseCore 0:
  207.0 26.0 reduce-scatter.1
where the time goes:
time: 244 us; the launch traced here: 240 us
  matrix products  92 us (38%)
  waiting for transfers between devices  41.2 us (17%)
  local copies, waits for them, and re-layouts  32.3 us (13%)
  starting transfers between devices  30.5 us (12%)
  between operations  24.8 us (10%)
  other arithmetic  19.3 us (8%)
    dot_general x2, matrix products, shards(): jnp.einsum('hts,shd->thd', (scores * mixing).astype(jnp.bfloat16), value_...  26.8 us
    reduce_scatter x1, waiting for transfers between devices, shards(): lax.psum_scatter(jnp.dot(attended, w_out, preferred_element_type=jnp.floa...  26.2 us
    ppermute x11, starting transfers between devices, swapped(): return lax.ppermute(block, axis, route)  22.9 us
    dot_general x14, matrix products, shards(): jnp.einsum('thd,hde->the', query_float, states_stack[level_id], precision...  22.5 us
    sub x2, matrix products, shards(): exponents = jnp.exp(logits - row_peak)  19.2 us
    ppermute x11, waiting for transfers between devices, swapped(): return lax.ppermute(block, axis, route)  15 us
    dot_general x2, matrix products, shards(): jnp.einsum('kgts,skd->tkgd', window_weights, value_window, preferred_elem...  14.3 us
    unnamed x112, local copies, waits for them, and re-layouts  14 us
  transfers between devices with their start and end apart: 14, of which 8 were waited for; matrix products, arithmetic and copies ran while one was open for 52% of the time, Pallas kernels for 0%

commit v1 on v0

v1 whole, which is shorter than its diff:
```python
import functools
import math

import jax
import jax.numpy as jnp
from jax import lax
from jax.experimental import pallas as pl
from jax.experimental.pallas import tpu as pltpu
from jax.sharding import PartitionSpec as P

DH = 128
TILE = 256
EPSILON = 1e-06
SCORE_SCALE = DH ** (-0.5) * math.log2(math.e)
F32 = jnp.float32
BF16 = jnp.bfloat16


def nt(a, b):
    return lax.dot_general(a, b, (((1,), (1,)), ((), ())), preferred_element_type=F32)


def nn(a, b):
    return jnp.dot(a, b, preferred_element_type=F32)


def head_weights(index, table_ref, head):
    weights = jnp.zeros(index.shape, F32)
    for row in range(table_ref.shape[0]):
        weights = jnp.where(index == row, table_ref[row, head], weights)
    level = lax.broadcasted_iota(jnp.int32, (index.shape[0], 1), 0).astype(F32)
    return weights * jnp.exp2(-0.5 * level)


def level_pattern(size):
    s = lax.broadcasted_iota(jnp.int32, (size, size), 0)
    t = lax.broadcasted_iota(jnp.int32, (size, size), 1)
    level = jnp.zeros((size, size), jnp.int32)
    differ = s ^ t
    for bit in range(size.bit_length() - 1):
        level = level + (differ >= (1 << bit)).astype(jnp.int32)
    return jnp.where(s <= t, level, -1)


def near_tile(q, k, vt, rows, pattern):
    half = TILE // 2
    left = nt(k[:half], q)
    right = nt(k[half:], q[half:])
    mix_left = jnp.zeros((half, half), F32)
    mix_right = jnp.zeros((half, half), F32)
    for level in range(8):
        row = rows(level)
        hit = pattern == level
        mix_left = jnp.where(hit, row[:, :half], mix_left)
        mix_right = jnp.where(hit, row[:, half:], mix_right)
    top = jnp.concatenate(
        [(left[:, :half] * mix_left).astype(BF16), (left[:, half:] * rows(8)[:, half:]).astype(BF16)], axis=1
    )
    bottom = jnp.concatenate([jnp.zeros((half, half), BF16), (right * mix_right).astype(BF16)], axis=1)
    return nn(vt, jnp.concatenate([top, bottom], axis=0))


def window_tile(q, keys, vt, current, penalty):
    scores = nt(keys, q)
    previous = scores[:TILE]
    if penalty is not None:
        previous = previous + penalty
    folded = jnp.where(current, scores[TILE:], previous)
    peak = jnp.max(folded, axis=0, keepdims=True)
    exps = jnp.exp2((folded - peak) * SCORE_SCALE)
    total = jnp.sum(exps, axis=0, keepdims=True)
    exps = exps.astype(BF16)
    zero = jnp.zeros_like(exps)
    probs = jnp.concatenate([jnp.where(current, zero, exps), jnp.where(current, exps, zero)], axis=0)
    raw = nn(vt, probs)
    inverse = 1.0 / total
    mean_square = jnp.mean(raw * raw, axis=0, keepdims=True) * (inverse * inverse)
    return raw * (inverse * lax.rsqrt(mean_square + EPSILON))


def states_kernel(k_ref, v_ref, tile_ref, shard_ref):
    total = None
    for tile in range(k_ref.shape[0] // TILE):
        span = pl.ds(tile * TILE, TILE)
        state = nn(v_ref[span, :].T, k_ref[span, :])
        tile_ref[0, tile] = state
        total = state if total is None else total + state
    shard_ref[0] = total


def middle_kernel(
    table_ref, opens_ref, q_ref, k_ref, v_ref, wk_ref, wv_ref, index_ref, tile_ref, gain_ref, near_ref, win_ref, far_w_ref
):
    head = pl.program_id(0)
    weights = head_weights(index_ref[...], table_ref, head)
    far_w_ref[0] = weights
    pattern = level_pattern(TILE // 2)
    s = lax.broadcasted_iota(jnp.int32, (TILE, TILE), 0)
    t = lax.broadcasted_iota(jnp.int32, (TILE, TILE), 1)
    current = s <= t
    gain = gain_ref[0].reshape(DH, 1)
    penalty = -1e30 * opens_ref[0].astype(F32)
    for tile in range(q_ref.shape[0] // TILE):
        first = tile * TILE
        span = pl.ds(first, TILE)
        q, k, vt = q_ref[span, :], k_ref[span, :], v_ref[span, :].T

        def rows(level):
            return weights[level : level + 1, first : first + TILE]

        near = near_tile(q, k, vt, rows, pattern)
        if tile % 2:
            near = near + rows(9) * nt(tile_ref[0, tile - 1].astype(BF16), q)
        if tile >= 2:
            near = near + rows(10) * nt((tile_ref[0, 0] + tile_ref[0, 1]).astype(BF16), q)
        near_ref[0, :, span] = near
        wide = pl.ds(first, 2 * TILE)
        win = window_tile(q, wk_ref[wide, :], wv_ref[wide, :].T, current, penalty if tile == 0 else None)
        win_ref[0, :, span] = win * gain


def last_kernel(keep_ref, q_ref, near_ref, win_ref, w_ref, bucket_ref, gain_ref, w_out_ref, out_ref):
    heads, stages = near_ref.shape[0], bucket_ref.shape[0]
    parts = []
    for head in range(heads):
        q = q_ref[:, head * DH : (head + 1) * DH]
        lin = near_ref[head]
        for stage in range(stages):
            row = w_ref[head, 11 + stage : 12 + stage, :] * keep_ref[stage]
            lin = lin + row * nt(bucket_ref[stage, head], q)
        mean_square = jnp.mean(lin * lin, axis=0, keepdims=True)
        lin = lin * lax.rsqrt(mean_square + EPSILON) * gain_ref[head].reshape(DH, 1)
        parts.append((lin + win_ref[head]).astype(BF16).T)
    attended = jnp.concatenate(parts, axis=1)
    out_ref[...] = nn(attended, w_out_ref[...]).astype(BF16)


def shards(
    queries,
    lin_keys,
    lin_values,
    window_keys,
    window_values,
    level_index,
    level_table,
    seq_lengths,
    gain_linear,
    gain_window,
    w_out,
):
    tokens = queries.shape[0]
    heads = level_table.shape[1]
    groups = window_keys.shape[1] // DH
    members = heads // groups
    levels = level_index.shape[0]
    tiles = tokens // TILE
    shard_count = lax.axis_size("seq")
    stages = shard_count.bit_length() - 1
    shard_id = lax.axis_index("seq")
    seq_starts = jnp.cumsum(seq_lengths) - seq_lengths
    seq_begin = jnp.max(jnp.where(seq_starts <= shard_id, seq_starts, 0))
    opens_here = (seq_begin == shard_id).astype(jnp.int32).reshape(1)

    route = [(i, i + 1) for i in range(shard_count - 1)]
    rim_keys, rim_values = lax.ppermute(
        (window_keys[tokens - TILE :], window_values[tokens - TILE :]), "seq", route
    )
    keys_ext = jnp.concatenate([rim_keys, window_keys], axis=0)
    values_ext = jnp.concatenate([rim_values, window_values], axis=0)

    column = lambda h: (0, h)
    tile_states, running = pl.pallas_call(
        states_kernel,
        grid=(heads,),
        in_specs=[pl.BlockSpec((tokens, DH), column)] * 2,
        out_specs=[
            pl.BlockSpec((1, tiles, DH, DH), lambda h: (h, 0, 0, 0)),
            pl.BlockSpec((1, DH, DH), lambda h: (h, 0, 0)),
        ],
        out_shape=[
            jax.ShapeDtypeStruct((heads, tiles, DH, DH), F32),
            jax.ShapeDtypeStruct((heads, DH, DH), F32),
        ],
        cost_estimate=pl.CostEstimate(flops=2 * tokens * DH * DH * heads, bytes_accessed=8 << 20, transcendentals=0),
    )(lin_keys, lin_values)

    near, win, weights = pl.pallas_call(
        middle_kernel,
        grid=(heads,),
        in_specs=[
            pl.BlockSpec(memory_space=pltpu.SMEM),
            pl.BlockSpec(memory_space=pltpu.SMEM),
            pl.BlockSpec((tokens, DH), column),
            pl.BlockSpec((tokens, DH), column),
            pl.BlockSpec((tokens, DH), column),
            pl.BlockSpec((tokens + TILE, DH), lambda h: (0, h // members)),
            pl.BlockSpec((tokens + TILE, DH), lambda h: (0, h // members)),
            pl.BlockSpec((levels, tokens), lambda h: (0, 0)),
            pl.BlockSpec((1, tiles, DH, DH), lambda h: (h, 0, 0, 0)),
            pl.BlockSpec((1, 1, DH), lambda h: (h, 0, 0)),
        ],
        out_specs=[
            pl.BlockSpec((1, DH, tokens), lambda h: (h, 0, 0)),
            pl.BlockSpec((1, DH, tokens), lambda h: (h, 0, 0)),
            pl.BlockSpec((1, levels, tokens), lambda h: (h, 0, 0)),
        ],
        out_shape=[
            jax.ShapeDtypeStruct((heads, DH, tokens), F32),
            jax.ShapeDtypeStruct((heads, DH, tokens), F32),
            jax.ShapeDtypeStruct((heads, levels, tokens), F32),
        ],
        cost_estimate=pl.CostEstimate(flops=4 << 30, bytes_accessed=20 << 20, transcendentals=4 << 20),
    )(
        level_table,
        opens_here,
        queries,
        lin_keys,
        lin_values,
        keys_ext,
        values_ext,
        level_index,
        tile_states,
        gain_window.reshape(heads, 1, DH),
    )

    buckets, keeps = [], []
    for stage in range(stages):
        span = 1 << stage
        mask = span | (span >> 1 if stage % 2 else 0)
        partner = lax.ppermute(running.astype(BF16), "seq", [(i, i ^ mask) for i in range(shard_count)])
        buckets.append(partner)
        base = shard_id // span * span
        upper = (shard_id // span) % 2 == 1
        other = jnp.where(upper, base - span, base + span)
        opened = jnp.any((seq_starts >= base) & (seq_starts < base + span))
        partner_opened = jnp.any((seq_starts >= other) & (seq_starts < other + span))
        keeps.append((upper & (seq_begin < base)).astype(F32))
        own_scale = jnp.where(upper | jnp.logical_not(partner_opened), 1.0, 0.0)
        partner_scale = jnp.where(upper & opened, 0.0, 1.0)
        running = own_scale * running + partner_scale * partner.astype(F32)

    rows = 256
    partial = pl.pallas_call(
        last_kernel,
        grid=(tokens // rows,),
        in_specs=[
            pl.BlockSpec(memory_space=pltpu.SMEM),
            pl.BlockSpec((rows, heads * DH), lambda i: (i, 0)),
            pl.BlockSpec((heads, DH, rows), lambda i: (0, 0, i)),
            pl.BlockSpec((heads, DH, rows), lambda i: (0, 0, i)),
            pl.BlockSpec((heads, levels, rows), lambda i: (0, 0, i)),
            pl.BlockSpec((stages, heads, DH, DH), lambda i: (0, 0, 0, 0)),
            pl.BlockSpec((heads, 1, DH), lambda i: (0, 0, 0)),
            pl.BlockSpec((heads * DH, w_out.shape[1]), lambda i: (0, 0)),
        ],
        out_specs=pl.BlockSpec((rows, w_out.shape[1]), lambda i: (i, 0)),
        out_shape=jax.ShapeDtypeStruct((tokens, w_out.shape[1]), BF16),
        compiler_params=pltpu.CompilerParams(vmem_limit_bytes=48 << 20),
        cost_estimate=pl.CostEstimate(flops=8 << 30, bytes_accessed=20 << 20, transcendentals=0),
    )(
        jnp.stack(keeps),
        queries,
        near,
        win,
        weights,
        jnp.stack(buckets),
        gain_linear.reshape(heads, 1, DH),
        w_out,
    )
    return lax.psum_scatter(partial, "head", scatter_dimension=0, tiled=True)


def solution(mesh):
    placed = (
        P("seq", "head"),
        P("seq", "head"),
        P("seq", "head"),
        P("seq", "head"),
        P("seq", "head"),
        P(None, "seq"),
        P(None, "head"),
        P(),
        P("head"),
        P("head"),
        P("head", None),
    )
    return jax.shard_map(
        shards, mesh=mesh, in_specs=placed, out_specs=P(("seq", "head"), None), check_vma=False
    )
```

time: 244 us -> 122 us (0.50); the launches traced: 240 us -> 121 us
  matrix products: 92 us -> 0 us
  Pallas kernels: 0 us -> 37.8 us
  local copies, waits for them, and re-layouts: 32.3 us -> 0.36 us
  starting transfers between devices: 30.5 us -> 18 us
  other arithmetic: 19.3 us -> 7.05 us
  waiting for transfers between devices: 41.2 us -> 33.8 us
    dot_general x21 -> x0, matrix products: 72.7 us -> none  [the longest x2 26.8 us: shards(): jnp.einsum('hts,shd->thd', (scores * mixing).astype(jnp.bfloat16), value_...]
    pallas_call x0 -> x3, Pallas kernels: none -> 37.8 us  [the longest x1 18.2 us: shards(): pl.pallas_call(middle_kernel, grid=(heads,), in_specs=[pl.BlockSpec(memor...]
    sub x2 -> x0, matrix products: 19.2 us -> none  [shards(): exponents = jnp.exp(logits - row_peak)]
    slice x14 -> x2, local copies, waits for them, and re-layouts: 14.9 us -> 0.02 us  [the longest x1 0.01 us: shards(): window_keys[tokens - TILE:]]
    unnamed x112 -> x19, local copies, waits for them, and re-layouts: 14 us -> 0.19 us
    ppermute x13 -> x8, starting transfers between devices: 30.5 us -> 18 us  [the longest x6 14.1 us: shards(): lax.ppermute(running.astype(BF16), 'seq', [(i, i ^ mask) for i in range(s...]
    select_n x5 -> x0, other arithmetic: 8.68 us -> none  [shards(): jnp.where(level_grid == level_id, 1.0, 0.0)[None, :, :]]
    reduce_scatter x1, waiting for transfers between devices: 26.2 us -> 21 us  [shards(): return lax.psum_scatter(partial, 'head', scatter_dimension=0, tiled=True)]
  transfers between devices with their start and end apart: 14 -> 9, of which waited for: 8 -> 5; matrix products, arithmetic and copies ran while one was open for 52% -> 4% of each run, Pallas kernels for 0% -> 15%
where the time goes in v1:
time: 122 us; the launch traced here: 121 us
  Pallas kernels  37.8 us (31%)
  waiting for transfers between devices  33.8 us (28%)
  between operations  24.3 us (20%)
  starting transfers between devices  18 us (15%)
  other arithmetic  7.05 us (6%)
    reduce_scatter x1, waiting for transfers between devices, shards(): return lax.psum_scatter(partial, 'head', scatter_dimension=0, tiled=True)  21 us
    pallas_call x1, Pallas kernels, shards(): pl.pallas_call(middle_kernel, grid=(heads,), in_specs=[pl.BlockSpec(memor...  18.2 us
    ppermute x6, starting transfers between devices, shards(): lax.ppermute(running.astype(BF16), 'seq', [(i, i ^ mask) for i in range(s...  14.1 us
    ppermute x6, waiting for transfers between devices, shards(): lax.ppermute(running.astype(BF16), 'seq', [(i, i ^ mask) for i in range(s...  12.8 us
    pallas_call x1, Pallas kernels, shards(): pl.pallas_call(last_kernel, grid=(tokens // rows,), in_specs=[pl.BlockSpe...  12.6 us
    pallas_call x1, Pallas kernels, shards(): pl.pallas_call(states_kernel, grid=(heads,), in_specs=[pl.BlockSpec((toke...  7.02 us
    ppermute x2, starting transfers between devices, shards(): lax.ppermute((window_keys[tokens - TILE:], window_values[tokens - TILE:])...  3.86 us
    convert_element_type x6, other arithmetic, shards(): running.astype(BF16)  2.97 us
  transfers between devices with their start and end apart: 9, of which 5 were waited for; matrix products, arithmetic and copies ran while one was open for 4% of the time, Pallas kernels for 15%

profile of v1, /device:TPU:1, one launch (start us, length us, event | category | flops | bytes accessed | tf_op | source)
XLA Modules:
  0.0 121.3 jit_solution(3423442994000059944)
XLA Ops:
  6.5 0.0 copy-start.6
  6.5 0.0 reduce-scatter.2.cloned.1.call-start
  6.5 7.0 %shard_map.109 = (f32[8,4,128,128]{3,2,1,0:T(8,128)}, f32[8,128,128]{2,1,0:T(8,128)}) custom-call(bf16[1024,1024]{1,0:T(8,128)(2,1)} %k_ref.3, bf16[1024,1024]{1,0:T(8,128)(2,1)} %v_ref.3), custom_call_target="tpu_custom_call" | custom-call | flops 268435456 | bytes 8388608 | tf_op jit(solution)/shard_map/pallas_call | solution.py:172
  13.6 0.0 copy-start.5
  13.6 0.0 copy-start.4
  13.6 0.0 copy-start.3
  13.6 1.2 convert_element_type.40
  14.8 2.2 %collective-permute-start.2 = (bf16[8,128,128]{2,1,0:T(8,128)(2,1)S(1)}, bf16[8,128,128]{2,1,0:T(8,128)(2,1)S(1)}, u32[]{:S(2)}, u32[]{:S(2)}) collective-permute-start(bf16[8,128,128]{2,1,0:T(8,128)(2,1)S(1)} %convert_element_type.40), channel_id=1, source_target_pairs={{0,2},{2,0},{4,6},{6,4},{8,10},{10,8},{12,14},{14,12},{16,18},{18,... | collective-permute-start | bytes 786440 | tf_op jit(solution)/shard_map/ppermute | solution.py:230
  17.0 0.0 copy-done.6
  17.0 0.2 reduce-window.9
  17.2 0.6 and_reduce_fusion
  17.8 0.8 and_reduce_fusion.1
  19.9 2.7 %collective-permute-done.2 = bf16[8,128,128]{2,1,0:T(8,128)(2,1)S(1)} collective-permute-done((bf16[8,128,128]{2,1,0:T(8,128)(2,1)S(1)}, bf16[8,128,128]{2,1,0:T(8,128)(2,1)S(1)}, u32[]{:S(2)}, u32[]{:S(2)}) %collective-permute-start.2) | collective-permute-done | bytes 262176 | tf_op jit(solution)/shard_map/ppermute | solution.py:230
  22.6 1.1 fusion
  23.7 3.1 %collective-permute-start.3 = (bf16[8,128,128]{2,1,0:T(8,128)(2,1)S(1)}, bf16[8,128,128]{2,1,0:T(8,128)(2,1)S(1)}, u32[]{:S(2)}, u32[]{:S(2)}) collective-permute-start(bf16[8,128,128]{2,1,0:T(8,128)(2,1)S(1)} %fusion), channel_id=1, source_target_pairs={{0,6},{2,4},{4,2},{6,0},{8,14},{10,12},{12,10},{14,8},{16,22},{18,... | collective-permute-start | bytes 786440 | tf_op jit(solution)/shard_map/ppermute | solution.py:230
  26.8 0.0 copy-done.5
  26.8 1.8 %collective-permute-start.1 = (bf16[256,256]{1,0:T(8,128)(2,1)S(1)}, bf16[256,256]{1,0:T(8,128)(2,1)S(1)}, u32[]{:S(2)}, u32[]{:S(2)}) collective-permute-start(bf16[256,256]{1,0:T(8,128)(2,1)S(1)} %slice.7), channel_id=1, source_target_pairs={{0,2},{2,4},{4,6},{6,8},{8,10},{10,12},{12,14},{14,16},{16,18},{18... | collective-permute-start | bytes 393224 | tf_op jit(solution)/shard_map/ppermute | solution.py:165
  28.6 0.0 copy-done.4
  28.6 2.1 %collective-permute-start = (bf16[256,256]{1,0:T(8,128)(2,1)S(1)}, bf16[256,256]{1,0:T(8,128)(2,1)S(1)}, u32[]{:S(2)}, u32[]{:S(2)}) collective-permute-start(bf16[256,256]{1,0:T(8,128)(2,1)S(1)} %slice.6), channel_id=1, source_target_pairs={{0,2},{2,4},{4,6},{6,8},{8,10},{10,12},{12,14},{14,16},{16,18},{18... | collective-permute-start | bytes 393224 | tf_op jit(solution)/shard_map/ppermute | solution.py:165
  30.8 0.6 fusion.3
  40.8 0.1 stack.56
  40.9 0.0 collective-permute-done.3
  40.9 0.0 copy-done.3
  40.9 0.2 fusion.4
  41.1 1.7 %collective-permute-start.4 = (bf16[8,128,128]{2,1,0:T(8,128)(2,1)S(1)}, bf16[8,128,128]{2,1,0:T(8,128)(2,1)S(1)}, u32[]{:S(2)}, u32[]{:S(2)}) collective-permute-start(bf16[8,128,128]{2,1,0:T(8,128)(2,1)S(1)} %get-tuple-element.26), channel_id=1, source_target_pairs={{0,8},{2,10},{4,12},{6,14},{8,0},{10,2},{12,4},{14,6},{16,24},{18,... | collective-permute-start | bytes 786440 | tf_op jit(solution)/shard_map/ppermute | solution.py:230
  42.8 0.0 collective-permute-done
  42.8 0.9 pad_maximum_fusion.wk_ref
  43.7 0.0 collective-permute-done.1
  43.7 0.9 pad_maximum_fusion.1.wv_ref
  44.6 2.4 %collective-permute-done.4 = bf16[8,128,128]{2,1,0:T(8,128)(2,1)S(1)} collective-permute-done((bf16[8,128,128]{2,1,0:T(8,128)(2,1)S(1)}, bf16[8,128,128]{2,1,0:T(8,128)(2,1)S(1)}, u32[]{:S(2)}, u32[]{:S(2)}) %collective-permute-start.4) | collective-permute-done | bytes 262176 | tf_op jit(solution)/shard_map/ppermute | solution.py:230
  47.0 0.1 fusion.1
  47.0 3.3 %collective-permute-start.5 = (bf16[8,128,128]{2,1,0:T(8,128)(2,1)S(1)}, bf16[8,128,128]{2,1,0:T(8,128)(2,1)S(1)}, u32[]{:S(2)}, u32[]{:S(2)}) collective-permute-start(bf16[8,128,128]{2,1,0:T(8,128)(2,1)S(1)} %fusion.1), channel_id=1, source_target_pairs={{0,24},{2,26},{4,28},{6,30},{8,16},{10,18},{12,20},{14,22},{16,8},... | collective-permute-start | bytes 786440 | tf_op jit(solution)/shard_map/ppermute | solution.py:230
  50.3 18.2 %shard_map.110 = (f32[8,128,1024]{2,1,0:T(8,128)}, f32[8,128,1024]{2,1,0:T(8,128)}, f32[8,17,1024]{2,1,0:T(8,128)}) custom-call(f32[8,8]{1,0:T(8,128)} %table_ref.1, s32[1]{0:T(128)} %bitcast.8.opens_ref, bf16[1024,1024]{1,0:T(8,128)(2,1)} %q_ref.3, bf16[1024,1024]{1,0:T(8,128)(2,1)} %k_ref.3, bf16[1024,1024]{1,0:T(8,128)(2,1)} %v_ref.3, ...), custom_call_target="tpu_custom_call" | custom-call | flops 4294967296 | bytes 20971520 | tf_op jit(solution)/shard_map/pallas_call | solution.py:187
  68.5 0.0 collective-permute-done.5
  68.5 0.2 fusion.2
  68.7 1.3 %collective-permute-start.6 = (bf16[8,128,128]{2,1,0:T(8,128)(2,1)S(1)}, bf16[8,128,128]{2,1,0:T(8,128)(2,1)S(1)}, u32[]{:S(2)}, u32[]{:S(2)}) collective-permute-start(bf16[8,128,128]{2,1,0:T(8,128)(2,1)S(1)} %fusion.2), channel_id=1, source_target_pairs={{0,32},{2,34},{4,36},{6,38},{8,40},{10,42},{12,44},{14,46},{16,48}... | collective-permute-start | bytes 786440 | tf_op jit(solution)/shard_map/ppermute | solution.py:230
  70.1 0.0 copy-start
  70.1 0.0 copy-start.1
  70.1 0.0 copy-start.2
  70.1 3.9 %collective-permute-done.6 = bf16[8,128,128]{2,1,0:T(8,128)(2,1)S(1)} collective-permute-done((bf16[8,128,128]{2,1,0:T(8,128)(2,1)S(1)}, bf16[8,128,128]{2,1,0:T(8,128)(2,1)S(1)}, u32[]{:S(2)}, u32[]{:S(2)}) %collective-permute-start.6) | collective-permute-done | bytes 262176 | tf_op jit(solution)/shard_map/ppermute | solution.py:230
  74.0 0.2 add_convert_fusion
  74.2 2.6 %collective-permute-start.7 = (bf16[8,128,128]{2,1,0:T(8,128)(2,1)S(1)}, bf16[8,128,128]{2,1,0:T(8,128)(2,1)S(1)}, u32[]{:S(2)}, u32[]{:S(2)}) collective-permute-start(bf16[8,128,128]{2,1,0:T(8,128)(2,1)S(1)} %add_convert_fusion), channel_id=1, source_target_pairs={{0,96},{2,98},{4,100},{6,102},{8,104},{10,106},{12,108},{14,110},{... | collective-permute-start | bytes 786440 | tf_op jit(solution)/shard_map/ppermute | solution.py:230
  76.9 3.9 %collective-permute-done.7 = bf16[8,128,128]{2,1,0:T(8,128)(2,1)S(1)} collective-permute-done((bf16[8,128,128]{2,1,0:T(8,128)(2,1)S(1)}, bf16[8,128,128]{2,1,0:T(8,128)(2,1)S(1)}, u32[]{:S(2)}, u32[]{:S(2)}) %collective-permute-start.7) | collective-permute-done | bytes 262176 | tf_op jit(solution)/shard_map/ppermute | solution.py:230
  80.8 0.0 copy-done
  80.8 0.0 copy-done.1
  80.8 0.0 copy-done.2
  80.8 12.6 %shard_map.111 = bf16[1024,2048]{1,0:T(8,128)(2,1)} custom-call(f32[6]{0:T(128)S(1)} %stack.57.keep_ref, bf16[1024,1024]{1,0:T(8,128)(2,1)S(1)} %copy-done, f32[8,128,1024]{2,1,0:T(8,128)} %get-tuple-element.11.near_ref, f32[8,128,1024]{2,1,0:T(8,128)} %get-tuple-element.12.win_ref, f32[8,17,1024]{2,1,0:T(8,128)S(1)} %copy-done.2, ...), custom_call_target="tpu_custom_call" | custom-call | flops 8589934592 | bytes 20971520 | tf_op jit(solution)/shard_map/pallas_call | solution.py:243
  93.4 0.0 reduce-scatter.2.cloned.1.call-update
  93.4 21.0 %reduce-scatter.2.cloned.1.call-done = bf16[512,2048]{1,0:T(8,128)(2,1)} async-done(((bf16[1024,2048]{1,0:T(8,128)(2,1)}), bf16[512,2048]{1,0:T(8,128)(2,1)}) %reduce-scatter.2.cloned.1.call-update) | async-done | bytes 2097168 | tf_op jit(solution)/shard_map/reduce_scatter | solution.py:270
  (9 shorter events, 0.2 us)
Async XLA Ops:
  6.5 10.4 %copy-start.6 = (s32[4]{0:T(128)S(1)}, s32[4]{0:T(128)}, u32[]{:S(2)}) copy-start(s32[4]{0:T(128)} %param.18) | copy-start | bytes 52
  6.5 107.9 %reduce-scatter.2.cloned.1.call-start = ((), (), s32[]{:S(2)}) async-start(), calls=%async_computation.1 | async-start | bytes 6291456 | tf_op jit(solution)/shard_map/reduce_scatter | solution.py:270
  13.6 13.3 %copy-start.5 = (bf16[1024,256]{1,0:T(8,128)(2,1)S(1)}, bf16[1024,256]{1,0:T(8,128)(2,1)}, u32[]{:S(2)}) copy-start(bf16[1024,256]{1,0:T(8,128)(2,1)} %param.15) | copy-start | bytes 1572868
  13.6 15.1 %copy-start.4 = (bf16[1024,256]{1,0:T(8,128)(2,1)S(1)}, bf16[1024,256]{1,0:T(8,128)(2,1)}, u32[]{:S(2)}) copy-start(bf16[1024,256]{1,0:T(8,128)(2,1)} %param.14) | copy-start | bytes 1572868
  13.6 27.4 %copy-start.3 = (f32[8,128,128]{2,1,0:T(8,128)S(1)}, f32[8,128,128]{2,1,0:T(8,128)}, u32[]{:S(2)}) copy-start(f32[8,128,128]{2,1,0:T(8,128)} %get-tuple-element.14) | copy-start | bytes 1572868
  14.8 7.8 %collective-permute-start.2 = (bf16[8,128,128]{2,1,0:T(8,128)(2,1)S(1)}, bf16[8,128,128]{2,1,0:T(8,128)(2,1)S(1)}, u32[]{:S(2)}, u32[]{:S(2)}) collective-permute-start(bf16[8,128,128]{2,1,0:T(8,128)(2,1)S(1)} %convert_element_type.40), channel_id=1, source_target_pairs={{0,2},{2,0},{4,6},{6,4},{8,10},{10,8},{12,14},{14,12},{16,18},{18,... | collective-permute-start | bytes 786440 | tf_op jit(solution)/shard_map/ppermute | solution.py:230
  23.7 17.2 %collective-permute-start.3 = (bf16[8,128,128]{2,1,0:T(8,128)(2,1)S(1)}, bf16[8,128,128]{2,1,0:T(8,128)(2,1)S(1)}, u32[]{:S(2)}, u32[]{:S(2)}) collective-permute-start(bf16[8,128,128]{2,1,0:T(8,128)(2,1)S(1)} %fusion), channel_id=1, source_target_pairs={{0,6},{2,4},{4,2},{6,0},{8,14},{10,12},{12,10},{14,8},{16,22},{18,... | collective-permute-start | bytes 786440 | tf_op jit(solution)/shard_map/ppermute | solution.py:230
  26.8 16.9 %collective-permute-start.1 = (bf16[256,256]{1,0:T(8,128)(2,1)S(1)}, bf16[256,256]{1,0:T(8,128)(2,1)S(1)}, u32[]{:S(2)}, u32[]{:S(2)}) collective-permute-start(bf16[256,256]{1,0:T(8,128)(2,1)S(1)} %slice.7), channel_id=1, source_target_pairs={{0,2},{2,4},{4,6},{6,8},{8,10},{10,12},{12,14},{14,16},{16,18},{18... | collective-permute-start | bytes 393224 | tf_op jit(solution)/shard_map/ppermute | solution.py:165
  28.6 14.2 %collective-permute-start = (bf16[256,256]{1,0:T(8,128)(2,1)S(1)}, bf16[256,256]{1,0:T(8,128)(2,1)S(1)}, u32[]{:S(2)}, u32[]{:S(2)}) collective-permute-start(bf16[256,256]{1,0:T(8,128)(2,1)S(1)} %slice.6), channel_id=1, source_target_pairs={{0,2},{2,4},{4,6},{6,8},{8,10},{10,12},{12,14},{14,16},{16,18},{18... | collective-permute-start | bytes 393224 | tf_op jit(solution)/shard_map/ppermute | solution.py:165
  41.1 5.9 %collective-permute-start.4 = (bf16[8,128,128]{2,1,0:T(8,128)(2,1)S(1)}, bf16[8,128,128]{2,1,0:T(8,128)(2,1)S(1)}, u32[]{:S(2)}, u32[]{:S(2)}) collective-permute-start(bf16[8,128,128]{2,1,0:T(8,128)(2,1)S(1)} %get-tuple-element.26), channel_id=1, source_target_pairs={{0,8},{2,10},{4,12},{6,14},{8,0},{10,2},{12,4},{14,6},{16,24},{18,... | collective-permute-start | bytes 786440 | tf_op jit(solution)/shard_map/ppermute | solution.py:230
  47.0 21.5 %collective-permute-start.5 = (bf16[8,128,128]{2,1,0:T(8,128)(2,1)S(1)}, bf16[8,128,128]{2,1,0:T(8,128)(2,1)S(1)}, u32[]{:S(2)}, u32[]{:S(2)}) collective-permute-start(bf16[8,128,128]{2,1,0:T(8,128)(2,1)S(1)} %fusion.1), channel_id=1, source_target_pairs={{0,24},{2,26},{4,28},{6,30},{8,16},{10,18},{12,20},{14,22},{16,8},... | collective-permute-start | bytes 786440 | tf_op jit(solution)/shard_map/ppermute | solution.py:230
  68.7 5.3 %collective-permute-start.6 = (bf16[8,128,128]{2,1,0:T(8,128)(2,1)S(1)}, bf16[8,128,128]{2,1,0:T(8,128)(2,1)S(1)}, u32[]{:S(2)}, u32[]{:S(2)}) collective-permute-start(bf16[8,128,128]{2,1,0:T(8,128)(2,1)S(1)} %fusion.2), channel_id=1, source_target_pairs={{0,32},{2,34},{4,36},{6,38},{8,40},{10,42},{12,44},{14,46},{16,48}... | collective-permute-start | bytes 786440 | tf_op jit(solution)/shard_map/ppermute | solution.py:230
  70.1 10.7 %copy-start = (bf16[1024,1024]{1,0:T(8,128)(2,1)S(1)}, bf16[1024,1024]{1,0:T(8,128)(2,1)}, u32[]{:S(2)}) copy-start(bf16[1024,1024]{1,0:T(8,128)(2,1)} %q_ref.3) | copy-start | bytes 6291460
  70.1 10.7 %copy-start.1 = (f32[1024]{0:T(1024)S(1)}, f32[1024]{0:T(1024)}, u32[]{:S(2)}) copy-start(f32[1024]{0:T(1024)} %param.19) | copy-start | bytes 12292
  70.1 10.7 %copy-start.2 = (f32[8,17,1024]{2,1,0:T(8,128)S(1)}, f32[8,17,1024]{2,1,0:T(8,128)}, u32[]{:S(2)}) copy-start(f32[8,17,1024]{2,1,0:T(8,128)} %get-tuple-element.13.w_ref) | copy-start | bytes 1671172
  74.2 6.5 %collective-permute-start.7 = (bf16[8,128,128]{2,1,0:T(8,128)(2,1)S(1)}, bf16[8,128,128]{2,1,0:T(8,128)(2,1)S(1)}, u32[]{:S(2)}, u32[]{:S(2)}) collective-permute-start(bf16[8,128,128]{2,1,0:T(8,128)(2,1)S(1)} %add_convert_fusion), channel_id=1, source_target_pairs={{0,96},{2,98},{4,100},{6,102},{8,104},{10,106},{12,108},{14,110},{... | collective-permute-start | bytes 786440 | tf_op jit(solution)/shard_map/ppermute | solution.py:230
Sparse Core Ops, SparseCore 0:
  93.6 20.8 reduce-scatter.1

commit v2 on v1

v2 whole, which is shorter than its diff:
```python
import math

import jax
import jax.numpy as jnp
from jax import lax
from jax.experimental import pallas as pl
from jax.experimental.pallas import tpu as pltpu
from jax.sharding import PartitionSpec as P

DH = 128
TILE = 256
EPSILON = 1e-06
SCORE_SCALE = DH ** (-0.5) * math.log2(math.e)
F32 = jnp.float32
BF16 = jnp.bfloat16
MESH = pl.DeviceIdType.MESH
LAG = 2


def nt(a, b):
    return lax.dot_general(a, b, (((1,), (1,)), ((), ())), preferred_element_type=F32)


def nn(a, b):
    return jnp.dot(a, b, preferred_element_type=F32)


def head_weights(index, table_ref, head):
    weights = jnp.zeros(index.shape, F32)
    for row in range(table_ref.shape[0]):
        weights = jnp.where(index == row, table_ref[row, head], weights)
    level = lax.broadcasted_iota(jnp.int32, (index.shape[0], 1), 0).astype(F32)
    return weights * jnp.exp2(-0.5 * level)


def level_pattern(size):
    s = lax.broadcasted_iota(jnp.int32, (size, size), 0)
    t = lax.broadcasted_iota(jnp.int32, (size, size), 1)
    level = jnp.zeros((size, size), jnp.int32)
    differ = s ^ t
    for bit in range(size.bit_length() - 1):
        level = level + (differ >= (1 << bit)).astype(jnp.int32)
    return jnp.where(s <= t, level, -1)


def near_tile(q, k, vt, rows, pattern):
    half = TILE // 2
    left = nt(k[:half], q)
    right = nt(k[half:], q[half:])
    mix_left = jnp.zeros((half, half), F32)
    mix_right = jnp.zeros((half, half), F32)
    for level in range(8):
        row = rows(level)
        hit = pattern == level
        mix_left = jnp.where(hit, row[:, :half], mix_left)
        mix_right = jnp.where(hit, row[:, half:], mix_right)
    top = jnp.concatenate(
        [(left[:, :half] * mix_left).astype(BF16), (left[:, half:] * rows(8)[:, half:]).astype(BF16)], axis=1
    )
    bottom = jnp.concatenate([jnp.zeros((half, half), BF16), (right * mix_right).astype(BF16)], axis=1)
    return nn(vt, jnp.concatenate([top, bottom], axis=0))


def window_tile(q, keys, vt, current, penalty):
    scores = nt(keys, q)
    previous = scores[:TILE]
    if penalty is not None:
        previous = previous + penalty
    folded = jnp.where(current, scores[TILE:], previous)
    peak = jnp.max(folded, axis=0, keepdims=True)
    exps = jnp.exp2((folded - peak) * SCORE_SCALE)
    total = jnp.sum(exps, axis=0, keepdims=True)
    exps = exps.astype(BF16)
    zero = jnp.zeros_like(exps)
    probs = jnp.concatenate([jnp.where(current, zero, exps), jnp.where(current, exps, zero)], axis=0)
    raw = nn(vt, probs)
    inverse = 1.0 / total
    mean_square = jnp.mean(raw * raw, axis=0, keepdims=True) * (inverse * inverse)
    return raw * (inverse * lax.rsqrt(mean_square + EPSILON))


def partner_of(shard, stage):
    unit = 4 ** (stage // 2)
    digit = shard // unit % 4
    other = 3 - digit if stage % 2 else digit + 1 - 2 * (digit % 2)
    return shard + (other - digit) * unit


def kernel(
    table_ref,
    lengths_ref,
    index_ref,
    gain_lin_ref,
    gain_win_ref,
    q_hbm,
    k_hbm,
    v_hbm,
    wk_hbm,
    wv_hbm,
    w_hbm,
    out_hbm,
    q_ref,
    k_ref,
    v_ref,
    vt_ref,
    wk_ref,
    wv_ref,
    wvt_ref,
    w_ref,
    weights_ref,
    tile_ref,
    run_ref,
    send_ref,
    recv_ref,
    lin_ref,
    win_ref,
    att_ref,
    part_ref,
    other_ref,
    kv_sem,
    q_sem,
    win_sem,
    w_sem,
    send_sem,
    recv_sem,
    rim_send_sem,
    rim_recv_sem,
    part_send_sem,
    part_recv_sem,
    out_sem,
):
    heads, tokens, _ = q_ref.shape
    groups = wk_ref.shape[0]
    members = heads // groups
    tiles = tokens // TILE
    stages = recv_ref.shape[1]
    own_rows = out_hbm.shape[0]
    own_tiles = own_rows // TILE
    shard_count = 1 << stages
    shard = lax.axis_index("seq")
    core = lax.axis_index("head")
    following = (shard + 1) % shard_count
    preceding = (shard + shard_count - 1) % shard_count

    def columns(hbm, h):
        return hbm.at[:, pl.ds(pl.multiple_of(h * DH, DH), DH)]

    def k_copy(h):
        return pltpu.make_async_copy(columns(k_hbm, h), k_ref.at[h], kv_sem.at[0, h])

    def v_copy(h):
        return pltpu.make_async_copy(columns(v_hbm, h), v_ref.at[h], kv_sem.at[1, h])

    def q_copy(h):
        return pltpu.make_async_copy(columns(q_hbm, h), q_ref.at[h], q_sem.at[h])

    def wk_copy(g):
        return pltpu.make_async_copy(columns(wk_hbm, g), wk_ref.at[g, pl.ds(TILE, tokens)], win_sem.at[0, g])

    def wv_copy(g):
        return pltpu.make_async_copy(columns(wv_hbm, g), wv_ref.at[g, pl.ds(TILE, tokens)], win_sem.at[1, g])

    w_copy = pltpu.make_async_copy(w_hbm, w_ref, w_sem)

    def hop(stage, h):
        return pltpu.make_async_remote_copy(
            src_ref=send_ref.at[stage, h],
            dst_ref=recv_ref.at[h, stage],
            send_sem=send_sem.at[stage, h],
            recv_sem=recv_sem.at[stage, h],
            device_id={"seq": partner_of(shard, stage)},
            device_id_type=MESH,
        )

    def rim(hbm, ref, which, g):
        return pltpu.make_async_remote_copy(
            src_ref=hbm.at[pl.ds(tokens - TILE, TILE), pl.ds(g * DH, DH)],
            dst_ref=ref.at[g, pl.ds(0, TILE)],
            send_sem=rim_send_sem.at[which, g],
            recv_sem=rim_recv_sem.at[which, g],
            device_id={"seq": following},
            device_id_type=MESH,
        )

    rims = [rim(wk_hbm, wk_ref, 0, g) for g in range(groups)] + [rim(wv_hbm, wv_ref, 1, g) for g in range(groups)]

    def part_copy(r):
        return pltpu.make_async_remote_copy(
            src_ref=part_ref.at[r],
            dst_ref=other_ref.at[r],
            send_sem=part_send_sem.at[r],
            recv_sem=part_recv_sem.at[r],
            device_id={"head": 1 - core},
            device_id_type=MESH,
        )

    def out_copy(r):
        return pltpu.make_async_copy(part_ref.at[own_tiles + r], out_hbm.at[pl.ds(r * TILE, TILE)], out_sem.at[r])

    for h in range(heads):
        k_copy(h).start()
        v_copy(h).start()
    for h in range(heads):
        q_copy(h).start()
    for g in range(groups):
        wk_copy(g).start()
        wv_copy(g).start()
    w_copy.start()

    barrier = pltpu.get_barrier_semaphore()
    for stage in range(stages):
        pl.semaphore_signal(barrier, inc=1, device_id={"seq": partner_of(shard, stage)}, device_id_type=MESH)
    pl.semaphore_signal(barrier, inc=1, device_id={"seq": preceding}, device_id_type=MESH)
    pl.semaphore_signal(barrier, inc=1, device_id={"head": 1 - core}, device_id_type=MESH)

    starts, begin, running_start = [], 0, 0
    for i in range(lengths_ref.shape[0]):
        starts.append(running_start)
        running_start = running_start + lengths_ref[i]
    for start in starts[1:]:
        begin = jnp.where(start <= shard, start, begin)
    opens_here = begin == shard

    def opened(base, span):
        found = False
        for start in starts:
            found = jnp.logical_or(found, jnp.logical_and(start >= base, start < base + span))
        return found

    keep, own_scale, partner_scale = [], [], []
    for stage in range(stages):
        span = 1 << stage
        base = shard // span * span
        upper = (shard // span) % 2 == 1
        other = jnp.where(upper, base - span, base + span)
        keep.append(jnp.where(jnp.logical_and(upper, begin < base), 1.0, 0.0))
        own_scale.append(jnp.where(jnp.logical_and(jnp.logical_not(upper), opened(other, span)), 0.0, 1.0))
        partner_scale.append(jnp.where(jnp.logical_and(upper, opened(base, span)), 0.0, 1.0))

    @pl.loop(0, heads)
    def _(h):
        weights_ref[h] = head_weights(index_ref[...], table_ref, h)

    pl.semaphore_wait(barrier, stages + 2)

    @pl.loop(0, heads)
    def _(h):
        k_copy(h).wait()
        v_copy(h).wait()
        vt_ref[h] = v_ref[h].T
        states = [
            nn(vt_ref[h, :, t * TILE : (t + 1) * TILE], k_ref[h, t * TILE : (t + 1) * TILE, :]) for t in range(tiles)
        ]
        pair = states[0] + states[1]
        tile_ref[h, 0] = states[0].astype(BF16)
        tile_ref[h, 1] = states[2].astype(BF16)
        tile_ref[h, 2] = pair.astype(BF16)
        total = pair + (states[2] + states[3])
        run_ref[h] = total
        send_ref[0, h] = total.astype(BF16)
        hop(0, h).start()

    for copy in rims:
        copy.start()

    def tick(n):
        for stage in range(stages - 1):
            h = n - LAG * stage

            @pl.when(jnp.logical_and(h >= 0, h < heads))
            def _():
                hop(stage, h).wait_recv()
                total = own_scale[stage] * run_ref[h] + partner_scale[stage] * recv_ref[h, stage].astype(F32)
                run_ref[h] = total
                send_ref[stage + 1, h] = total.astype(BF16)
                hop(stage + 1, h).start()

    for g in range(groups):
        wk_copy(g).wait()
        wv_copy(g).wait()
        wvt_ref[g, :, TILE:] = wv_ref[g, TILE:, :].T

    pattern = level_pattern(TILE // 2)
    s = lax.broadcasted_iota(jnp.int32, (TILE, TILE), 0)
    t = lax.broadcasted_iota(jnp.int32, (TILE, TILE), 1)
    current = s <= t

    def window(h, tile, penalty):
        first = tile * TILE
        g = h // members
        raw = window_tile(
            q_ref[h, first : first + TILE, :],
            wk_ref[g, first : first + 2 * TILE, :],
            wvt_ref[g, :, first : first + 2 * TILE],
            current,
            penalty,
        )
        win_ref[h, :, first : first + TILE] = raw * gain_win_ref[h].reshape(DH, 1)

    @pl.loop(0, heads)
    def _(h):
        q_copy(h).wait()
        for tile in range(tiles):
            first = tile * TILE
            q = q_ref[h, first : first + TILE, :]

            def rows(level):
                return weights_ref[h, level : level + 1, first : first + TILE]

            near = near_tile(q, k_ref[h, first : first + TILE, :], vt_ref[h, :, first : first + TILE], rows, pattern)
            if tile % 2:
                near = near + rows(9) * nt(tile_ref[h, tile // 2], q)
            if tile >= 2:
                near = near + rows(10) * nt(tile_ref[h, 2], q)
            lin_ref[h, :, first : first + TILE] = near
        tick(2 * h)
        for tile in range(1, tiles):
            window(h, tile, None)
        tick(2 * h + 1)

    for copy in rims:
        copy.wait_recv()
    for g in range(groups):
        wvt_ref[g, :, :TILE] = wv_ref[g, :TILE, :].T
    penalty = jnp.where(opens_here, -1e30, 0.0)

    @pl.loop(0, heads)
    def _(h):
        window(h, 0, penalty)

    w_copy.wait()

    @pl.loop(0, heads)
    def _(h):
        hop(stages - 1, h).wait_recv()

    @pl.loop(0, 2 * own_tiles)
    def _(r):
        mine = r // own_tiles
        first = pl.multiple_of((core + 1 - mine) % 2 * own_rows + r % own_tiles * TILE, TILE)
        span = pl.ds(first, TILE)
        for h in range(heads):
            q = q_ref[h, span, :]
            lin = lin_ref[h, :, span]
            far = nt(recv_ref[h].reshape(stages * DH, DH), q)
            for stage in range(stages):
                row = weights_ref[h, 11 + stage : 12 + stage, span] * keep[stage]
                lin = lin + row * far[stage * DH : (stage + 1) * DH]
            mean_square = jnp.mean(lin * lin, axis=0, keepdims=True)
            lin = lin * lax.rsqrt(mean_square + EPSILON) * gain_lin_ref[h].reshape(DH, 1)
            att_ref[:, h * DH : (h + 1) * DH] = (lin + win_ref[h, :, span]).astype(BF16).T
        part_ref[r] = nn(att_ref[...], w_ref[...]).astype(BF16)

        @pl.when(r < own_tiles)
        def _():
            part_copy(r).start()

        @pl.when(r >= own_tiles)
        def _():
            part_copy(r - own_tiles).wait_recv()
            part_ref[r] = (part_ref[r].astype(F32) + other_ref[r - own_tiles].astype(F32)).astype(BF16)
            out_copy(r - own_tiles).start()

    for copy in rims:
        copy.wait_send()

    @pl.loop(0, heads)
    def _(h):
        for stage in range(stages):
            hop(stage, h).wait_send()

    for r in range(own_tiles):
        part_copy(r).wait_send()
        out_copy(r).wait()


def shards(
    queries,
    lin_keys,
    lin_values,
    window_keys,
    window_values,
    level_index,
    level_table,
    seq_lengths,
    gain_linear,
    gain_window,
    w_out,
):
    tokens = queries.shape[0]
    heads = level_table.shape[1]
    groups = window_keys.shape[1] // DH
    levels = level_index.shape[0]
    tiles = tokens // TILE
    stages = lax.axis_size("seq").bit_length() - 1
    width = w_out.shape[1]
    own_rows = tokens // lax.axis_size("head")
    own_tiles = own_rows // TILE
    smem = pl.BlockSpec(memory_space=pltpu.SMEM)
    vmem = pl.BlockSpec(memory_space=pltpu.VMEM)
    hbm = pl.BlockSpec(memory_space=pl.ANY)
    dma = pltpu.SemaphoreType.DMA
    return pl.pallas_call(
        kernel,
        in_specs=[smem, smem, vmem, vmem, vmem] + [hbm] * 6,
        out_specs=hbm,
        out_shape=jax.ShapeDtypeStruct((own_rows, width), BF16),
        scratch_shapes=[
            pltpu.VMEM((heads, tokens, DH), BF16),
            pltpu.VMEM((heads, tokens, DH), BF16),
            pltpu.VMEM((heads, tokens, DH), BF16),
            pltpu.VMEM((heads, DH, tokens), BF16),
            pltpu.VMEM((groups, TILE + tokens, DH), BF16),
            pltpu.VMEM((groups, TILE + tokens, DH), BF16),
            pltpu.VMEM((groups, DH, TILE + tokens), BF16),
            pltpu.VMEM(w_out.shape, BF16),
            pltpu.VMEM((heads, levels, tokens), F32),
            pltpu.VMEM((heads, 3, DH, DH), BF16),
            pltpu.VMEM((heads, DH, DH), F32),
            pltpu.VMEM((stages, heads, DH, DH), BF16),
            pltpu.VMEM((heads, stages, DH, DH), BF16),
            pltpu.VMEM((heads, DH, tokens), F32),
            pltpu.VMEM((heads, DH, tokens), F32),
            pltpu.VMEM((TILE, heads * DH), BF16),
            pltpu.VMEM((2 * own_tiles, TILE, width), BF16),
            pltpu.VMEM((own_tiles, TILE, width), BF16),
            dma((2, heads)),
            dma((heads,)),
            dma((2, groups)),
            dma,
            dma((stages, heads)),
            dma((stages, heads)),
            dma((2, groups)),
            dma((2, groups)),
            dma((own_tiles,)),
            dma((own_tiles,)),
            dma((own_tiles,)),
        ],
        compiler_params=pltpu.CompilerParams(
            collective_id=0, has_side_effects=True, vmem_limit_bytes=60 << 20
        ),
    )(
        level_table,
        seq_lengths,
        level_index,
        gain_linear.reshape(heads, 1, DH),
        gain_window.reshape(heads, 1, DH),
        queries,
        lin_keys,
        lin_values,
        window_keys,
        window_values,
        w_out,
    )


def solution(mesh):
    placed = (
        P("seq", "head"),
        P("seq", "head"),
        P("seq", "head"),
        P("seq", "head"),
        P("seq", "head"),
        P(None, "seq"),
        P(None, "head"),
        P(),
        P("head"),
        P("head"),
        P("head", None),
    )
    return jax.shard_map(
        shards, mesh=mesh, in_specs=placed, out_specs=P(("seq", "head"), None), check_vma=False
    )
```

time: 122 us -> 59.4 us (0.49)
  waiting for transfers between devices: 33.8 us -> 0 us
  between operations: 24.3 us -> 0.01 us
  starting transfers between devices: 18 us -> 0 us
  Pallas kernels: 37.8 us -> 55.1 us
  other arithmetic: 7.05 us -> 0 us
  local copies, waits for them, and re-layouts: 0.36 us -> 3.16 us
    reduce_scatter x1 -> x0, waiting for transfers between devices: 21 us -> none  [shards(): return lax.psum_scatter(partial, 'head', scatter_dimension=0, tiled=True)]
    ppermute x8 -> x0, starting transfers between devices: 18 us -> none  [the longest x6 14.1 us: shards(): lax.ppermute(running.astype(BF16), 'seq', [(i, i ^ mask) for i in range(s...]
    pallas_call x3 -> x1, Pallas kernels: 37.8 us -> 55.1 us  [shards(): pl.pallas_call(kernel, in_specs=[smem, smem, vmem, vmem, vmem] + [hbm] *...]
    ppermute x8 -> x0, waiting for transfers between devices: 12.8 us -> none  [the longest x6 12.8 us: shards(): lax.ppermute(running.astype(BF16), 'seq', [(i, i ^ mask) for i in range(s...]
    convert_element_type x6 -> x0, other arithmetic: 2.97 us -> none  [shards(): running.astype(BF16)]
    unnamed x19 -> x1, local copies, waits for them, and re-layouts: 0.19 us -> 3.16 us
    concatenate x2 -> x0, other arithmetic: 1.78 us -> none  [the longest x1 0.9 us: shards(): keys_ext = jnp.concatenate([rim_keys, window_keys], axis=0)]
    reduce_or x2 -> x0, other arithmetic: 1.47 us -> none  [the longest x1 0.84 us: shards(): jnp.any((seq_starts >= other) & (seq_starts < other + span))]
  transfers between devices with their start and end apart: 9 -> 0, of which waited for: 5 -> 0; matrix products, arithmetic and copies ran while one was open for 4% -> 0% of each run, Pallas kernels for 15% -> 0%
where the time goes in v2:
time: 59.4 us; the launch traced here: 58.3 us
  Pallas kernels  55.1 us (93%)
  local copies, waits for them, and re-layouts  3.16 us (5%)
    pallas_call x1, Pallas kernels, shards(): pl.pallas_call(kernel, in_specs=[smem, smem, vmem, vmem, vmem] + [hbm] *...  55.1 us
    unnamed x1, local copies, waits for them, and re-layouts  3.16 us

profile of v2, /device:TPU:1, one launch (start us, length us, event | category | flops | bytes accessed | tf_op | source)
XLA Modules:
  0.0 58.3 jit_solution(10268559163715946776)
XLA Ops:
  0.0 55.1 %shard_map.109 = bf16[512,2048]{1,0:T(8,128)(2,1)} custom-call(f32[8,8]{1,0:T(8,128)} %table_ref.1, s32[4]{0:T(128)} %lengths_ref.1, s32[17,1024]{1,0:T(8,128)} %index_ref.1, f32[8,1,128]{2,1,0:T(1,128)} %bitcast.2, f32[8,1,128]{2,1,0:T(1,128)} %bitcast.3, bf16[1024,1024]{1,0:T(8,128)(2,1)} %q_hbm.1, bf16[1024,1024]{1,0:T(8,128)(2,1)} %k_hbm.1, ...), custom_call_target="tpu_custom_call" | custom-call | tf_op jit(solution)/shard_map/pallas_call | solution.py:403
  55.2 3.2 %copy.13 = bf16[512,2048]{1,0:T(8,128)(2,1)} copy(bf16[512,2048]{1,0:T(8,128)(2,1)} %shard_map.109) | data formatting | bytes 4194304

commit v3 on v2

v3 whole, which is shorter than its diff:
```python
import math

import jax
import jax.numpy as jnp
from jax import lax
from jax.experimental import pallas as pl
from jax.experimental.pallas import tpu as pltpu
from jax.sharding import PartitionSpec as P

DH = 128
TILE = 256
EPSILON = 1e-06
SCORE_SCALE = DH ** (-0.5) * math.log2(math.e)
F32 = jnp.float32
BF16 = jnp.bfloat16
MESH = pl.DeviceIdType.MESH
LAG = 6
RIM_PIECES = 4
RIM_X = 6
RIM_Y = 14


def nn(a, b):
    return jnp.dot(a, b, preferred_element_type=F32)


def head_weights(index, table_ref, head):
    weights = jnp.zeros(index.shape, F32)
    for row in range(table_ref.shape[0]):
        weights = jnp.where(index == row, table_ref[row, head], weights)
    level = lax.broadcasted_iota(jnp.int32, (index.shape[0], 1), 0).astype(F32)
    return weights * jnp.exp2(-0.5 * level)


def level_pattern(size):
    s = lax.broadcasted_iota(jnp.int32, (size, size), 0)
    t = lax.broadcasted_iota(jnp.int32, (size, size), 1)
    level = jnp.zeros((size, size), jnp.int32)
    differ = s ^ t
    for bit in range(size.bit_length() - 1):
        level = level + (differ >= (1 << bit)).astype(jnp.int32)
    return jnp.where(s <= t, level, -1)


def near_tile(qt, k, vt, rows, pattern):
    half = TILE // 2
    left = nn(k[:half], qt)
    right = nn(k[half:], qt[:, half:])
    mix_left = jnp.zeros((half, half), F32)
    mix_right = jnp.zeros((half, half), F32)
    for level in range(8):
        row = rows(level)
        hit = pattern == level
        mix_left = jnp.where(hit, row[:, :half], mix_left)
        mix_right = jnp.where(hit, row[:, half:], mix_right)
    top = jnp.concatenate(
        [(left[:, :half] * mix_left).astype(BF16), (left[:, half:] * rows(8)[:, half:]).astype(BF16)], axis=1
    )
    bottom = jnp.concatenate([jnp.zeros((half, half), BF16), (right * mix_right).astype(BF16)], axis=1)
    return nn(vt, jnp.concatenate([top, bottom], axis=0))


def window_rows(q, kt, v, current, penalty):
    n = q.shape[0]
    scores = nn(q.reshape(n * TILE, DH), kt).reshape(n, TILE, 2 * TILE)
    previous = scores[:, :, :TILE]
    if penalty is not None:
        previous = previous + penalty
    folded = jnp.where(current, scores[:, :, TILE:], previous)
    peak = jnp.max(folded, axis=2, keepdims=True)
    exps = jnp.exp2((folded - peak) * SCORE_SCALE)
    total = jnp.sum(exps, axis=2, keepdims=True)
    probs = jnp.concatenate([jnp.where(current, 0.0, exps), jnp.where(current, exps, 0.0)], axis=2).astype(BF16)
    raw = nn(probs.reshape(n * TILE, 2 * TILE), v).reshape(n, TILE, DH)
    inverse = 1.0 / total
    mean_square = jnp.mean(raw * raw, axis=2, keepdims=True) * (inverse * inverse)
    return raw * (inverse * lax.rsqrt(mean_square + EPSILON))


def partner_of(shard, stage):
    unit = 4 ** (stage // 2)
    digit = shard // unit % 4
    other = 3 - digit if stage % 2 else digit + 1 - 2 * (digit % 2)
    return shard + (other - digit) * unit


def kernel(
    table_ref,
    lengths_ref,
    index_ref,
    gain_lin_ref,
    gain_win_ref,
    q_hbm,
    k_hbm,
    v_hbm,
    wk_hbm,
    wv_hbm,
    w_hbm,
    own_hbm,
    other_hbm,
    q_ref,
    k_ref,
    v_ref,
    qt_ref,
    vt_ref,
    window_ref,
    wkt_ref,
    rim_ref,
    w_ref,
    weights_ref,
    tile_ref,
    run_ref,
    send_ref,
    recv_ref,
    lin_ref,
    win_ref,
    att_ref,
    part_ref,
    kv_sem,
    q_sem,
    win_sem,
    w_sem,
    send_sem,
    recv_sem,
    rim_load_sem,
    rim_send_sem,
    rim_recv_sem,
    part_send_sem,
    part_recv_sem,
    out_sem,
):
    heads, tokens, _ = q_ref.shape
    groups = window_ref.shape[1]
    members = heads // groups
    tiles = tokens // TILE
    stages = recv_ref.shape[1]
    own_rows = own_hbm.shape[0]
    own_tiles = own_rows // TILE
    shard = lax.axis_index("seq")
    core = lax.axis_index("head")

    def columns(hbm, h):
        return hbm.at[:, pl.ds(pl.multiple_of(h * DH, DH), DH)]

    def k_copy(h):
        return pltpu.make_async_copy(columns(k_hbm, h), k_ref.at[h], kv_sem.at[0, h])

    def v_copy(h):
        return pltpu.make_async_copy(columns(v_hbm, h), v_ref.at[h], kv_sem.at[1, h])

    def q_copy(h):
        return pltpu.make_async_copy(columns(q_hbm, h), q_ref.at[h], q_sem.at[h])

    def wk_copy(g):
        return pltpu.make_async_copy(columns(wk_hbm, g), window_ref.at[0, g, pl.ds(TILE, tokens)], win_sem.at[0, g])

    def wv_copy(g):
        return pltpu.make_async_copy(columns(wv_hbm, g), window_ref.at[1, g, pl.ds(TILE, tokens)], win_sem.at[1, g])

    w_copy = pltpu.make_async_copy(w_hbm, w_ref, w_sem)

    def hop(stage, h):
        return pltpu.make_async_remote_copy(
            src_ref=send_ref.at[stage, h],
            dst_ref=recv_ref.at[h, stage],
            send_sem=send_sem.at[stage, h],
            recv_sem=recv_sem.at[stage, h],
            device_id={"seq": partner_of(shard, stage)},
            device_id_type=MESH,
        )

    place = [shard % 4, shard // 4 % 4, shard // 16]
    rim_count = groups * RIM_PIECES
    last_y = place[0] == 3
    on_leg = [last_y, jnp.logical_and(last_y, place[1] == 0), place[0] >= 0]
    from_z = jnp.logical_and(last_y, place[1] > 0)
    rim_slot = jnp.where(on_leg[1], 2, jnp.where(last_y, 1, 0))

    def rim(leg, n):
        rows = TILE // RIM_PIECES
        g, piece = n // RIM_PIECES, n % RIM_PIECES
        span = pl.ds(pl.multiple_of(piece * rows, rows), rows)
        axis = (1, 2, 0)[leg]
        return pltpu.make_async_remote_copy(
            src_ref=rim_ref.at[(0, 1, rim_slot)[leg], :, g, span],
            dst_ref=rim_ref.at[leg + 1, :, g, span],
            send_sem=rim_send_sem.at[leg, n],
            recv_sem=rim_recv_sem.at[leg, n],
            device_id={"seq": shard + ((place[axis] + 1) % 4 - place[axis]) * 4**axis},
            device_id_type=MESH,
        )

    def rim_load(which, g):
        hbm = (wk_hbm, wv_hbm)[which]
        return pltpu.make_async_copy(
            hbm.at[pl.ds(tokens - TILE, TILE), pl.ds(g * DH, DH)], rim_ref.at[0, which, g], rim_load_sem.at[which, g]
        )

    def part_copy(r):
        return pltpu.make_async_remote_copy(
            src_ref=part_ref.at[r],
            dst_ref=other_hbm.at[pl.ds(r * TILE, TILE)],
            send_sem=part_send_sem.at[r],
            recv_sem=part_recv_sem.at[r],
            device_id={"head": 1 - core},
            device_id_type=MESH,
        )

    def out_copy(r):
        return pltpu.make_async_copy(part_ref.at[own_tiles + r], own_hbm.at[pl.ds(r * TILE, TILE)], out_sem.at[r])

    for h in range(heads):
        k_copy(h).start()
        v_copy(h).start()
    for g in range(groups):
        for which in range(2):
            rim_load(which, g).start()
    for h in range(heads):
        q_copy(h).start()
    for g in range(groups):
        wk_copy(g).start()
        wv_copy(g).start()
    w_copy.start()

    barrier = pltpu.get_barrier_semaphore()
    for stage in range(stages):
        pl.semaphore_signal(barrier, inc=1, device_id={"seq": partner_of(shard, stage)}, device_id_type=MESH)
    pl.semaphore_signal(barrier, inc=1, device_id={"head": 1 - core}, device_id_type=MESH)

    starts, begin, running_start = [], 0, 0
    for i in range(lengths_ref.shape[0]):
        starts.append(running_start)
        running_start = running_start + lengths_ref[i]
    for start in starts[1:]:
        begin = jnp.where(start <= shard, start, begin)
    opens_here = begin == shard

    def opened(base, span):
        found = False
        for start in starts:
            found = jnp.logical_or(found, jnp.logical_and(start >= base, start < base + span))
        return found

    keep, own_scale, partner_scale = [], [], []
    for stage in range(stages):
        span = 1 << stage
        base = shard // span * span
        upper = (shard // span) % 2 == 1
        other = jnp.where(upper, base - span, base + span)
        keep.append(jnp.where(jnp.logical_and(upper, begin < base), 1.0, 0.0))
        own_scale.append(jnp.where(jnp.logical_and(jnp.logical_not(upper), opened(other, span)), 0.0, 1.0))
        partner_scale.append(jnp.where(jnp.logical_and(upper, opened(base, span)), 0.0, 1.0))

    @pl.loop(0, heads)
    def _(h):
        weights_ref[h] = head_weights(index_ref[...], table_ref, h)

    for g in range(groups):
        for which in range(2):
            rim_load(which, g).wait()
    pl.semaphore_wait(barrier, stages + 1)

    @pl.when(on_leg[0])
    def _():
        @pl.loop(0, rim_count)
        def _(n):
            rim(0, n).start()


    @pl.loop(0, heads)
    def _(h):
        k_copy(h).wait()
        v_copy(h).wait()
        vt_ref[h] = v_ref[h].T
        states = [
            nn(vt_ref[h, :, t * TILE : (t + 1) * TILE], k_ref[h, t * TILE : (t + 1) * TILE, :]) for t in range(tiles)
        ]
        pair = states[0] + states[1]
        tile_ref[h, 0] = states[0].astype(BF16)
        tile_ref[h, 1] = states[2].astype(BF16)
        tile_ref[h, 2] = pair.astype(BF16)
        total = pair + (states[2] + states[3])
        run_ref[h] = total
        send_ref[0, h] = total.astype(BF16)
        hop(0, h).start()

    def tick(n):
        for stage in range(stages - 1):
            h = n - LAG * stage

            @pl.when(jnp.logical_and(h >= 0, h < heads))
            def _():
                hop(stage, h).wait_recv()
                total = own_scale[stage] * run_ref[h] + partner_scale[stage] * recv_ref[h, stage].astype(F32)
                run_ref[h] = total
                send_ref[stage + 1, h] = total.astype(BF16)
                hop(stage + 1, h).start()

        piece = n - RIM_X

        @pl.when(jnp.logical_and(on_leg[1], jnp.logical_and(piece >= 0, piece < rim_count)))
        def _():
            rim(0, piece).wait_recv()
            rim(1, piece).start()

        last = n - RIM_Y

        @pl.when(jnp.logical_and(last >= 0, last < rim_count))
        def _():
            @pl.when(from_z)
            def _():
                rim(0, last).wait_recv()

            @pl.when(on_leg[1])
            def _():
                rim(1, last).wait_recv()

            rim(2, last).start()

    for g in range(groups):
        wk_copy(g).wait()
        wv_copy(g).wait()
        for tile in range(1, tiles + 1):
            wkt_ref[g, tile] = window_ref[0, g, tile * TILE : (tile + 1) * TILE, :].T

    pattern = level_pattern(TILE // 2)
    t = lax.broadcasted_iota(jnp.int32, (TILE, TILE), 0)
    s = lax.broadcasted_iota(jnp.int32, (TILE, TILE), 1)
    current = s <= t

    def near(h, tile):
        first = tile * TILE
        qt = qt_ref[h, :, first : first + TILE]

        def rows(level):
            return weights_ref[h, level : level + 1, first : first + TILE]

        total = near_tile(qt, k_ref[h, first : first + TILE, :], vt_ref[h, :, first : first + TILE], rows, pattern)
        if tile % 2:
            total = total + rows(9) * nn(tile_ref[h, tile // 2], qt)
        if tile >= 2:
            total = total + rows(10) * nn(tile_ref[h, 2], qt)
        lin_ref[h, :, first : first + TILE] = total

    def window(g, tile, penalty):
        first = tile * TILE if isinstance(tile, int) else pl.multiple_of(tile * TILE, TILE)
        mine = pl.ds(g * members, members)
        raw = window_rows(
            q_ref[mine, pl.ds(first, TILE), :],
            jnp.concatenate([wkt_ref[g, tile], wkt_ref[g, tile + 1]], axis=1),
            window_ref[1, g, pl.ds(first, 2 * TILE), :],
            current,
            penalty,
        )
        win_ref[mine, pl.ds(first, TILE), :] = raw * gain_win_ref[mine]

    def far(h, tile, first_stage, last_stage):
        first = tile * TILE
        qt = qt_ref[h, :, first : first + TILE]
        count = last_stage - first_stage
        reached = nn(recv_ref[h, first_stage:last_stage].reshape(count * DH, DH), qt)
        lin = lin_ref[h, :, first : first + TILE]
        for i in range(count):
            level = 11 + first_stage + i
            row = weights_ref[h, level : level + 1, first : first + TILE] * keep[first_stage + i]
            lin = lin + row * reached[i * DH : (i + 1) * DH]
        return lin

    for h in range(heads):
        q_copy(h).wait()

    @pl.loop(0, heads)
    def _(i):
        qt_ref[i] = q_ref[i].T
        near(i, 0)
        near(i, 1)
        tick(3 * i)

        near(i, 2)
        near(i, 3)
        tick(3 * i + 1)

        @pl.when(i < groups * (tiles - 1))
        def _():
            window(i % groups, 1 + i // groups, None)

        tick(3 * i + 2)

    early = stages - 2

    @pl.loop(0, heads)
    def _(h):
        for tile in range(tiles):
            lin_ref[h, :, tile * TILE : (tile + 1) * TILE] = far(h, tile, 0, early)
        tick(3 * heads + h)

    @pl.loop(0, rim_count)
    def _(n):
        rim(2, n).wait_recv()

    for g in range(groups):
        wkt_ref[g, 0] = rim_ref[3, 0, g].T
        window_ref[1, g, :TILE, :] = rim_ref[3, 1, g]
        window(g, 0, jnp.where(opens_here, -1e30, 0.0))

    @pl.loop(0, heads)
    def _(h):
        hop(stages - 1, h).wait_recv()
        for tile in range(tiles):
            span = pl.ds(tile * TILE, TILE)
            lin = far(h, tile, early, stages)
            mean_square = jnp.mean(lin * lin, axis=0, keepdims=True)
            lin = (lin * lax.rsqrt(mean_square + EPSILON)).T * gain_lin_ref[h]
            att_ref[span, pl.ds(pl.multiple_of(h * DH, DH), DH)] = (lin + win_ref[h, span, :]).astype(BF16)

    w_copy.wait()

    @pl.loop(0, 2 * own_tiles)
    def _(r):
        mine = r // own_tiles
        first = pl.multiple_of((core + 1 - mine) % 2 * own_rows + r % own_tiles * TILE, TILE)
        part_ref[r] = nn(att_ref[pl.ds(first, TILE), :], w_ref[...]).astype(BF16)

        @pl.when(r < own_tiles)
        def _():
            part_copy(r).start()

        @pl.when(r >= own_tiles)
        def _():
            out_copy(r - own_tiles).start()

    for leg in range(3):

        @pl.when(on_leg[leg])
        def _():
            @pl.loop(0, rim_count)
            def _(n):
                rim(leg, n).wait_send()

    @pl.loop(0, heads)
    def _(h):
        for stage in range(stages):
            hop(stage, h).wait_send()

    for r in range(own_tiles):
        part_copy(r).wait()
        out_copy(r).wait()


def shards(
    queries,
    lin_keys,
    lin_values,
    window_keys,
    window_values,
    level_index,
    level_table,
    seq_lengths,
    gain_linear,
    gain_window,
    w_out,
):
    tokens = queries.shape[0]
    heads = level_table.shape[1]
    groups = window_keys.shape[1] // DH
    levels = level_index.shape[0]
    tiles = tokens // TILE
    stages = lax.axis_size("seq").bit_length() - 1
    width = w_out.shape[1]
    own_rows = tokens // lax.axis_size("head")
    own_tiles = own_rows // TILE
    smem = pl.BlockSpec(memory_space=pltpu.SMEM)
    vmem = pl.BlockSpec(memory_space=pltpu.VMEM)
    hbm = pl.BlockSpec(memory_space=pl.ANY)
    dma = pltpu.SemaphoreType.DMA
    own, other = pl.pallas_call(
        kernel,
        in_specs=[smem, smem, vmem, vmem, vmem] + [hbm] * 6,
        out_specs=[hbm] * 2,
        out_shape=[jax.ShapeDtypeStruct((own_rows, width), BF16)] * 2,
        scratch_shapes=[
            pltpu.VMEM((heads, tokens, DH), BF16),
            pltpu.VMEM((heads, tokens, DH), BF16),
            pltpu.VMEM((heads, tokens, DH), BF16),
            pltpu.VMEM((heads, DH, tokens), BF16),
            pltpu.VMEM((heads, DH, tokens), BF16),
            pltpu.VMEM((2, groups, TILE + tokens, DH), BF16),
            pltpu.VMEM((groups, tiles + 1, DH, TILE), BF16),
            pltpu.VMEM((4, 2, groups, TILE, DH), BF16),
            pltpu.VMEM(w_out.shape, BF16),
            pltpu.VMEM((heads, levels, tokens), F32),
            pltpu.VMEM((heads, 3, DH, DH), BF16),
            pltpu.VMEM((heads, DH, DH), F32),
            pltpu.VMEM((stages, heads, DH, DH), BF16),
            pltpu.VMEM((heads, stages, DH, DH), BF16),
            pltpu.VMEM((heads, DH, tokens), F32),
            pltpu.VMEM((heads, tokens, DH), F32),
            pltpu.VMEM((tokens, heads * DH), BF16),
            pltpu.VMEM((2 * own_tiles, TILE, width), BF16),
            dma((2, heads)),
            dma((heads,)),
            dma((2, groups)),
            dma,
            dma((stages, heads)),
            dma((stages, heads)),
            dma((2, groups)),
            dma((3, groups * RIM_PIECES)),
            dma((3, groups * RIM_PIECES)),
            dma((own_tiles,)),
            dma((own_tiles,)),
            dma((own_tiles,)),
        ],
        compiler_params=pltpu.CompilerParams(
            collective_id=0, has_side_effects=True, vmem_limit_bytes=60 << 20
        ),
    )(
        level_table,
        seq_lengths,
        level_index,
        gain_linear.reshape(heads, 1, DH),
        gain_window.reshape(heads, 1, DH),
        queries,
        lin_keys,
        lin_values,
        window_keys,
        window_values,
        w_out,
    )
    return (own.astype(F32) + other.astype(F32)).astype(BF16)


def solution(mesh):
    placed = (
        P("seq", "head"),
        P("seq", "head"),
        P("seq", "head"),
        P("seq", "head"),
        P("seq", "head"),
        P(None, "seq"),
        P(None, "head"),
        P(),
        P("head"),
        P("head"),
        P("head", None),
    )
    return jax.shard_map(
        shards, mesh=mesh, in_specs=placed, out_specs=P(("seq", "head"), None), check_vma=False
    )
```

time: 59.4 us -> 49.4 us (0.83); the launches traced: 58.3 us -> 49.3 us
  Pallas kernels: 55.1 us -> 44.8 us
  other arithmetic: 0 us -> 4.44 us
  local copies, waits for them, and re-layouts: 3.16 us -> 0 us
    pallas_call x1, Pallas kernels: 55.1 us -> 44.8 us  [shards(): pl.pallas_call(kernel, in_specs=[smem, smem, vmem, vmem, vmem] + [hbm] *...]
    convert_element_type x0 -> x1, other arithmetic: none -> 4.44 us  [shards(): return (own.astype(F32) + other.astype(F32)).astype(BF16)]
    unnamed x1 -> x0, local copies, waits for them, and re-layouts: 3.16 us -> none
where the time goes in v3:
time: 49.4 us; the launch traced here: 49.3 us
  Pallas kernels  44.8 us (91%)
  other arithmetic  4.44 us (9%)
    pallas_call x1, Pallas kernels, shards(): pl.pallas_call(kernel, in_specs=[smem, smem, vmem, vmem, vmem] + [hbm] *...  44.8 us
    convert_element_type x1, other arithmetic, shards(): return (own.astype(F32) + other.astype(F32)).astype(BF16)  4.44 us

profile of v3, /device:TPU:1, one launch (start us, length us, event | category | flops | bytes accessed | tf_op | source)
XLA Modules:
  0.0 49.3 jit_solution(11482807661313991930)
XLA Ops:
  0.0 44.8 %shard_map.109 = (bf16[512,2048]{1,0:T(8,128)(2,1)}, bf16[512,2048]{1,0:T(8,128)(2,1)}) custom-call(f32[8,8]{1,0:T(8,128)} %table_ref.1, s32[4]{0:T(128)} %lengths_ref.1, s32[17,1024]{1,0:T(8,128)} %index_ref.1, f32[8,1,128]{2,1,0:T(1,128)} %bitcast.2, f32[8,1,128]{2,1,0:T(1,128)} %bitcast.3, bf16[1024,1024]{1,0:T(8,128)(2,1)} %q_hbm.1, ...), custom_call_target="tpu_custom_call" | custom-call | tf_op jit(solution)/shard_map/pallas_call | solution.py:476
  44.8 4.4 %add_convert_fusion = bf16[512,2048]{1,0:T(8,128)(2,1)} fusion(bf16[512,2048]{1,0:T(8,128)(2,1)} %get-tuple-element.8, bf16[512,2048]{1,0:T(8,128)(2,1)} %get-tuple-element.7), kind=kLoop, calls=%fused_computation | loop fusion | flops 4194304 | bytes 6291456 | tf_op jit(solution)/shard_map/convert_element_type | solution.py:529

commit v4 on v3

--- a/solution.py
+++ b/solution.py
@@ -85,19 +85,24 @@
 
 
 def kernel(
-    table_ref,
-    lengths_ref,
-    index_ref,
-    gain_lin_ref,
-    gain_win_ref,
+    table_hbm,
+    lengths_hbm,
+    index_hbm,
+    gain_lin_hbm,
+    gain_win_hbm,
     q_hbm,
     k_hbm,
     v_hbm,
     wk_hbm,
     wv_hbm,
     w_hbm,
-    own_hbm,
-    other_hbm,
+    own_ref,
+    other_ref,
+    table_ref,
+    lengths_ref,
+    index_ref,
+    gain_lin_ref,
+    gain_win_ref,
     q_ref,
     k_ref,
     v_ref,
@@ -116,6 +121,7 @@
     win_ref,
     att_ref,
     part_ref,
+    small_sem,
     kv_sem,
     q_sem,
     win_sem,
@@ -127,14 +133,13 @@
     rim_recv_sem,
     part_send_sem,
     part_recv_sem,
-    out_sem,
 ):
     heads, tokens, _ = q_ref.shape
     groups = window_ref.shape[1]
     members = heads // groups
     tiles = tokens // TILE
     stages = recv_ref.shape[1]
-    own_rows = own_hbm.shape[0]
+    own_rows = own_ref.shape[0]
     own_tiles = own_rows // TILE
     shard = lax.axis_index("seq")
     core = lax.axis_index("head")
@@ -199,19 +204,30 @@
     def part_copy(r):
         return pltpu.make_async_remote_copy(
             src_ref=part_ref.at[r],
-            dst_ref=other_hbm.at[pl.ds(r * TILE, TILE)],
+            dst_ref=other_ref.at[pl.ds(r * TILE, TILE)],
             send_sem=part_send_sem.at[r],
             recv_sem=part_recv_sem.at[r],
             device_id={"head": 1 - core},
             device_id_type=MESH,
         )
 
-    def out_copy(r):
-        return pltpu.make_async_copy(part_ref.at[own_tiles + r], own_hbm.at[pl.ds(r * TILE, TILE)], out_sem.at[r])
-
+    small = [
+        pltpu.make_async_copy(hbm, ref, small_sem.at[n])
+        for n, (hbm, ref) in enumerate(
+            (
+                (lengths_hbm, lengths_ref),
+                (table_hbm, table_ref),
+                (index_hbm, index_ref),
+                (gain_lin_hbm, gain_lin_ref),
+                (gain_win_hbm, gain_win_ref),
+            )
+        )
+    ]
     for h in range(heads):
         k_copy(h).start()
         v_copy(h).start()
+    for copy in small:
+        copy.start()
     for g in range(groups):
         for which in range(2):
             rim_load(which, g).start()
@@ -227,48 +243,7 @@
         pl.semaphore_signal(barrier, inc=1, device_id={"seq": partner_of(shard, stage)}, device_id_type=MESH)
     pl.semaphore_signal(barrier, inc=1, device_id={"head": 1 - core}, device_id_type=MESH)
 
-    starts, begin, running_start = [], 0, 0
-    for i in range(lengths_ref.shape[0]):
-        starts.append(running_start)
-        running_start = running_start + lengths_ref[i]
-    for start in starts[1:]:
-        begin = jnp.where(start <= shard, start, begin)
-    opens_here = begin == shard
-
-    def opened(base, span):
-        found = False
-        for start in starts:
-            found = jnp.logical_or(found, jnp.logical_and(start >= base, start < base + span))
-        return found
-
-    keep, own_scale, partner_scale = [], [], []
-    for stage in range(stages):
-        span = 1 << stage
-        base = shard // span * span
-        upper = (shard // span) % 2 == 1
-        other = jnp.where(upper, base - span, base + span)
-        keep.append(jnp.where(jnp.logical_and(upper, begin < base), 1.0, 0.0))
-        own_scale.append(jnp.where(jnp.logical_and(jnp.logical_not(upper), opened(other, span)), 0.0, 1.0))
-        partner_scale.append(jnp.where(jnp.logical_and(upper, opened(base, span)), 0.0, 1.0))
-
-    @pl.loop(0, heads)
-    def _(h):
-        weights_ref[h] = head_weights(index_ref[...], table_ref, h)
-
-    for g in range(groups):
-        for which in range(2):
-            rim_load(which, g).wait()
-    pl.semaphore_wait(barrier, stages + 1)
-
-    @pl.when(on_leg[0])
-    def _():
-        @pl.loop(0, rim_count)
-        def _(n):
-            rim(0, n).start()
-
-
-    @pl.loop(0, heads)
-    def _(h):
+    def state(h):
         k_copy(h).wait()
         v_copy(h).wait()
         vt_ref[h] = v_ref[h].T
@@ -282,7 +257,56 @@
         total = pair + (states[2] + states[3])
         run_ref[h] = total
         send_ref[0, h] = total.astype(BF16)
+
+    state(0)
+    pl.semaphore_wait(barrier, stages + 1)
+    hop(0, 0).start()
+
+    @pl.loop(1, heads)
+    def _(h):
+        state(h)
         hop(0, h).start()
+
+    for g in range(groups):
+        for which in range(2):
+            rim_load(which, g).wait()
+
+    @pl.when(on_leg[0])
+    def _():
+        @pl.loop(0, rim_count)
+        def _(n):
+            rim(0, n).start()
+
+    for copy in small:
+        copy.wait()
+
+    starts, begin, running_start = [], 0, 0
+    for i in range(lengths_ref.shape[0]):
+        starts.append(running_start)
+        running_start = running_start + lengths_ref[i]
+    for start in starts[1:]:
+        begin = jnp.where(start <= shard, start, begin)
+    opens_here = begin == shard
+
+    def opened(base, span):
+        found = False
+        for start in starts:
+            found = jnp.logical_or(found, jnp.logical_and(start >= base, start < base + span))
+        return found
+
+    keep, own_scale, partner_scale = [], [], []
+    for stage in range(stages):
+        span = 1 << stage
+        base = shard // span * span
+        upper = (shard // span) % 2 == 1
+        other = jnp.where(upper, base - span, base + span)
+        keep.append(jnp.where(jnp.logical_and(upper, begin < base), 1.0, 0.0))
+        own_scale.append(jnp.where(jnp.logical_and(jnp.logical_not(upper), opened(other, span)), 0.0, 1.0))
+        partner_scale.append(jnp.where(jnp.logical_and(upper, opened(base, span)), 0.0, 1.0))
+
+    @pl.loop(0, heads)
+    def _(h):
+        weights_ref[h] = head_weights(index_ref[...], table_ref, h)
 
     def tick(n):
         for stage in range(stages - 1):
@@ -415,19 +439,18 @@
 
     w_copy.wait()
 
-    @pl.loop(0, 2 * own_tiles)
+    def project(owner, r):
+        first = pl.multiple_of(owner * own_rows + r * TILE, TILE)
+        return nn(att_ref[pl.ds(first, TILE), :], w_ref[...]).astype(BF16)
+
+    @pl.loop(0, own_tiles)
     def _(r):
-        mine = r // own_tiles
-        first = pl.multiple_of((core + 1 - mine) % 2 * own_rows + r % own_tiles * TILE, TILE)
-        part_ref[r] = nn(att_ref[pl.ds(first, TILE), :], w_ref[...]).astype(BF16)
-
-        @pl.when(r < own_tiles)
-        def _():
-            part_copy(r).start()
-
-        @pl.when(r >= own_tiles)
-        def _():
-            out_copy(r - own_tiles).start()
+        part_ref[r] = project(1 - core, r)
+        part_copy(r).start()
+
+    @pl.loop(0, own_tiles)
+    def _(r):
+        own_ref[pl.ds(pl.multiple_of(r * TILE, TILE), TILE), :] = project(core, r)
 
     for leg in range(3):
 
@@ -444,7 +467,6 @@
 
     for r in range(own_tiles):
         part_copy(r).wait()
-        out_copy(r).wait()
 
 
 def shards(
@@ -469,16 +491,20 @@
     width = w_out.shape[1]
     own_rows = tokens // lax.axis_size("head")
     own_tiles = own_rows // TILE
-    smem = pl.BlockSpec(memory_space=pltpu.SMEM)
     vmem = pl.BlockSpec(memory_space=pltpu.VMEM)
-    hbm = pl.BlockSpec(memory_space=pl.ANY)
+    hbm = pl.BlockSpec(memory_space=pltpu.HBM)
     dma = pltpu.SemaphoreType.DMA
     own, other = pl.pallas_call(
         kernel,
-        in_specs=[smem, smem, vmem, vmem, vmem] + [hbm] * 6,
-        out_specs=[hbm] * 2,
-        out_shape=[jax.ShapeDtypeStruct((own_rows, width), BF16)] * 2,
+        in_specs=[hbm] * 11,
+        out_specs=[vmem] * 2,
+        out_shape=[pltpu.VMEM((own_rows, width), BF16)] * 2,
         scratch_shapes=[
+            pltpu.SMEM(level_table.shape, F32),
+            pltpu.SMEM(seq_lengths.shape, jnp.int32),
+            pltpu.VMEM(level_index.shape, jnp.int32),
+            pltpu.VMEM((heads, 1, DH), F32),
+            pltpu.VMEM((heads, 1, DH), F32),
             pltpu.VMEM((heads, tokens, DH), BF16),
             pltpu.VMEM((heads, tokens, DH), BF16),
             pltpu.VMEM((heads, tokens, DH), BF16),
@@ -496,7 +522,8 @@
             pltpu.VMEM((heads, DH, tokens), F32),
             pltpu.VMEM((heads, tokens, DH), F32),
             pltpu.VMEM((tokens, heads * DH), BF16),
-            pltpu.VMEM((2 * own_tiles, TILE, width), BF16),
+            pltpu.VMEM((own_tiles, TILE, width), BF16),
+            dma((5,)),
             dma((2, heads)),
             dma((heads,)),
             dma((2, groups)),
@@ -508,23 +535,27 @@
             dma((3, groups * RIM_PIECES)),
             dma((own_tiles,)),
             dma((own_tiles,)),
-            dma((own_tiles,)),
         ],
         compiler_params=pltpu.CompilerParams(
-            collective_id=0, has_side_effects=True, vmem_limit_bytes=60 << 20
+            collective_id=0, has_side_effects=True, vmem_limit_bytes=48 << 20
         ),
     )(
-        level_table,
-        seq_lengths,
-        level_index,
-        gain_linear.reshape(heads, 1, DH),
-        gain_window.reshape(heads, 1, DH),
-        queries,
-        lin_keys,
-        lin_values,
-        window_keys,
-        window_values,
-        w_out,
+        *(
+            pltpu.with_memory_space_constraint(x, pltpu.HBM)
+            for x in (
+                level_table,
+                seq_lengths,
+                level_index,
+                gain_linear.reshape(heads, 1, DH),
+                gain_window.reshape(heads, 1, DH),
+                queries,
+                lin_keys,
+                lin_values,
+                window_keys,
+                window_values,
+                w_out,
+            )
+        )
     )
     return (own.astype(F32) + other.astype(F32)).astype(BF16)
 

time: 49.4 us -> 45.7 us (0.925)
  other arithmetic: 4.44 us -> 2.24 us
  Pallas kernels: 44.8 us -> 43.4 us
    convert_element_type x1, other arithmetic: 4.44 us -> 2.24 us  [shards(): return (own.astype(F32) + other.astype(F32)).astype(BF16)]
    pallas_call x1, Pallas kernels: 44.8 us -> 43.4 us  [shards(): pl.pallas_call(kernel, in_specs=[hbm] * 11, out_specs=[vmem] * 2, out_sha...]
where the time goes in v4:
time: 45.7 us; the launch traced here: 45.6 us
  Pallas kernels  43.4 us (95%)
  other arithmetic  2.24 us (5%)
    pallas_call x1, Pallas kernels, shards(): pl.pallas_call(kernel, in_specs=[hbm] * 11, out_specs=[vmem] * 2, out_sha...  43.4 us
    convert_element_type x1, other arithmetic, shards(): return (own.astype(F32) + other.astype(F32)).astype(BF16)  2.24 us

profile of v4, /device:TPU:1, one launch (start us, length us, event | category | flops | bytes accessed | tf_op | source)
XLA Modules:
  0.0 45.6 jit_solution(7368654058722483164)
XLA Ops:
  0.0 43.4 %shard_map.109 = (bf16[512,2048]{1,0:T(8,128)(2,1)S(1)}, bf16[512,2048]{1,0:T(8,128)(2,1)S(1)}) custom-call(f32[8,8]{1,0:T(8,128)} %table_hbm.1, s32[4]{0:T(128)} %lengths_hbm.1, s32[17,1024]{1,0:T(8,128)} %index_hbm.1, f32[8,1,128]{2,1,0:T(1,128)} %bitcast.2, f32[8,1,128]{2,1,0:T(1,128)} %bitcast.3, bf16[1024,1024]{1,0:T(8,128)(2,1)} %q_hbm.1, ...), custom_call_target="tpu_custom_call" | custom-call | tf_op jit(solution)/shard_map/pallas_call | solution.py:497
  43.4 2.2 %add_convert_fusion = bf16[512,2048]{1,0:T(8,128)(2,1)} fusion(bf16[512,2048]{1,0:T(8,128)(2,1)S(1)} %get-tuple-element.8, bf16[512,2048]{1,0:T(8,128)(2,1)S(1)} %get-tuple-element.7), kind=kLoop, calls=%fused_computation | loop fusion | flops 4194304 | bytes 6291456 | tf_op jit(solution)/shard_map/convert_element_type | solution.py:560

commit v5 on v4

--- a/solution.py
+++ b/solution.py
@@ -15,7 +15,7 @@
 BF16 = jnp.bfloat16
 MESH = pl.DeviceIdType.MESH
 LAG = 6
-RIM_PIECES = 4
+RIM_PIECES = 2
 RIM_X = 6
 RIM_Y = 14
 

time: 45.7 us -> 45.4 us (level)
  no operation moved by 1% of the time
where the time goes in v5:
time: 45.4 us; the launch traced here: 45.3 us
  Pallas kernels  43.1 us (95%)
  other arithmetic  2.24 us (5%)
    pallas_call x1, Pallas kernels, shards(): pl.pallas_call(kernel, in_specs=[hbm] * 11, out_specs=[vmem] * 2, out_sha...  43.1 us
    convert_element_type x1, other arithmetic, shards(): return (own.astype(F32) + other.astype(F32)).astype(BF16)  2.24 us

profile of v5, /device:TPU:1, one launch (start us, length us, event | category | flops | bytes accessed | tf_op | source)
XLA Modules:
  0.0 45.3 jit_solution(44253752309106878)
XLA Ops:
  0.0 43.1 %shard_map.109 = (bf16[512,2048]{1,0:T(8,128)(2,1)S(1)}, bf16[512,2048]{1,0:T(8,128)(2,1)S(1)}) custom-call(f32[8,8]{1,0:T(8,128)} %table_hbm.1, s32[4]{0:T(128)} %lengths_hbm.1, s32[17,1024]{1,0:T(8,128)} %index_hbm.1, f32[8,1,128]{2,1,0:T(1,128)} %bitcast.2, f32[8,1,128]{2,1,0:T(1,128)} %bitcast.3, bf16[1024,1024]{1,0:T(8,128)(2,1)} %q_hbm.1, ...), custom_call_target="tpu_custom_call" | custom-call | tf_op jit(solution)/shard_map/pallas_call | solution.py:497
  43.1 2.2 %add_convert_fusion = bf16[512,2048]{1,0:T(8,128)(2,1)} fusion(bf16[512,2048]{1,0:T(8,128)(2,1)S(1)} %get-tuple-element.8, bf16[512,2048]{1,0:T(8,128)(2,1)S(1)} %get-tuple-element.7), kind=kLoop, calls=%fused_computation | loop fusion | flops 4194304 | bytes 6291456 | tf_op jit(solution)/shard_map/convert_element_type | solution.py:560
